TPU v7x, 256 devices: a whole 4x4x8 slice. The times are simulated.
256 devices in a mesh: tp: 16 (over x, z_lo), hb: 16 (over y, z_hi, core).
Axes of the slice: x: 4, y: 4, z: 8 (z_hi: 2, z_lo: 4; z = z_hi * 4 + z_lo), core: 2. Of those that a mesh axis runs over, the one named last changes fastest.
Arguments:
- normed: bfloat16 [2048, 16384], P('hb', 'tp'), may hold values from -6 to 6
- hidden: bfloat16 [2048, 26624], P('hb', 'tp'), may hold values from -6 to 6
Outputs:
- h_in: float32 [16384, 16384], P('tp', 'hb')
- h_down: float32 [26624, 1664], P(('tp', 'hb'))
All inputs are finite; a program needn't handle non-finite values.
Results may differ from a plain program's by a relative error of at most 0.0003.
Values may be sent and summed in bfloat16 or wider, within the bound.
No kernel may reach another device: no remote copies, remote signals or barrier semaphores. Data moves between devices by JAX's collectives and lax.ppermute only.
A program may use at most 128 MiB of HBM per device.

v0:
```python
import jax
import jax.numpy as jnp
from jax import lax
from jax.sharding import PartitionSpec as P


def gram_product(left, right):
    return lax.dot_general(
        left, right, (((0,), (0,)), ((), ())), preferred_element_type=jnp.float32
    )


def per_device(normed, hidden):
    groups = lax.axis_size("hb")
    scale = 2.0 / (normed.shape[0] * groups)
    whole_rows = lax.all_gather(normed, "tp", axis=1, tiled=True)
    columns = lax.all_to_all(whole_rows, "hb", split_axis=1, concat_axis=0, tiled=True)
    part = columns
    h_in = gram_product(lax.all_gather(normed, "hb", axis=0, tiled=True), part) * scale
    part = hidden
    h_down = (
        lax.psum_scatter(gram_product(part, hidden), "hb", scatter_dimension=0, tiled=True) * scale
    )
    return (h_in, h_down)


def solution(mesh):
    return jax.shard_map(
        per_device,
        mesh=mesh,
        in_specs=(P("hb", "tp"), P("hb", "tp")),
        out_specs=(P("tp", "hb"), P(("tp", "hb"), None)),
        check_vma=False,
    )
```

profile of v0, /device:TPU:33, one launch (start us, length us, event | category | flops | bytes accessed | tf_op | source)
XLA Modules:
  0.0 416.4 jit_solution(16098393865919439729)
XLA Ops:
  7.2 0.0 copy-start
  7.2 0.0 all-gather.5.cloned.1.call-start
  7.2 1.8 copy.6
  9.1 0.0 all-gather.5.cloned.1.call-update
  9.1 0.0 all-gather.3.cloned.1.call-start
  9.1 0.7 all-gather.3.cloned.1.call-update
  9.8 0.0 reduce-scatter.4.cloned.1.call-start
  9.9 0.0 copy-done
  9.9 5.8 %fusion = f32[1664,1664]{1,0:T(8,128)} fusion(bf16[128,1664]{1,0:T(8,128)(2,1)S(1)} %copy-done), kind=kOutput, calls=%fused_computation.2 | convolution fusion | flops 708837376 | bytes 11501568 | tf_op jit(solution)/shard_map/dot_general | solution.py:8
  15.7 0.0 reduce-scatter.4.cloned.1.call-update
  15.8 95.4 %all-gather.5.cloned.1.call-done = bf16[128,16384]{0,1:T(8,128)(2,1)} async-done(((bf16[128,1024]{0,1:T(8,128)(2,1)}), bf16[128,16384]{0,1:T(8,128)(2,1)}) %all-gather.5.cloned.1.call-update) | async-done | bytes 4194320 | tf_op jit(solution)/shard_map/all_gather | solution.py:16
  111.2 109.2 %all_to_all.19 = bf16[128,16,1024]{0,2,1:T(8,128)(2,1)} all-to-all(bf16[128,16,1024]{0,2,1:T(8,128)(2,1)} %bitcast.9), channel_id=1, replica_groups=mesh['tp'=16,'hb'=16] {'hb'}, dimensions={1} | all-to-all | bytes 8388608 | tf_op jit(solution)/shard_map/all_to_all | solution.py:17
  220.3 6.4 %copy.7 = bf16[16,128,1024]{2,1,0:T(8,128)(2,1)} copy(bf16[16,128,1024]{1,2,0:T(8,128)(2,1)} %bitcast.8) | data formatting | bytes 8388608 | tf_op jit(solution)/shard_map/all_to_all | solution.py:17
  226.7 0.0 all-gather.3.cloned.1.call-done
  226.7 10.0 %convolution_multiply_fusion = f32[1024,1024]{1,0:T(8,128)} fusion(bf16[2048,1024]{1,0:T(8,128)(2,1)} %all-gather.3.cloned.1.call-done, bf16[2048,1024]{1,0:T(8,128)(2,1)} %bitcast.10), kind=kOutput, calls=%fused_computation | convolution fusion | flops 4296015872 | bytes 12582912 | tf_op jit(solution)/shard_map/dot_general | solution.py:8
  236.8 171.1 %reduce-scatter.4.cloned.1.call-done = f32[104,1664]{1,0:T(8,128)} async-done(((f32[1664,1664]{1,0:T(8,128)}), f32[104,1664]{1,0:T(8,128)}) %reduce-scatter.4.cloned.1.call-update) | async-done | bytes 692240
  407.9 2.0 broadcast_multiply_fusion
Async XLA Ops:
  7.2 2.7 copy-start
  7.2 104.0 %all-gather.5.cloned.1.call-start = ((), (), s32[]{:S(2)}) async-start(), calls=%async_computation.3 | async-start | bytes 4456448 | tf_op jit(solution)/shard_map/all_gather | solution.py:16
  9.1 217.6 %all-gather.3.cloned.1.call-start = ((), (), s32[]{:S(2)}) async-start(), calls=%async_computation.2 | async-start | bytes 4456448 | tf_op jit(solution)/shard_map/all_gather | solution.py:19
  9.8 398.1 %reduce-scatter.4.cloned.1.call-start = ((), (), s32[]{:S(2)}) async-start(), calls=%async_computation.4 | async-start | bytes 11767808
Sparse Core Ops, SparseCore 0:
  10.4 100.7 all-gather.4
  113.9 104.8 all-gather.2
  223.3 184.5 reduce-scatter.3
where the time goes:
time: 420 us; the launch traced here: 416 us
  waiting for transfers between devices  267 us (64%)
  blocking collectives  109 us (26%)
  matrix products  15.9 us (4%)
  between operations  13.8 us (3%)
  local copies, waits for them, and re-layouts  8.23 us (2%)
    unnamed x4, waiting for transfers between devices  172 us
    all_to_all x1, blocking collectives, per_device(): lax.all_to_all(whole_rows, 'hb', split_axis=1, concat_axis=0, tiled=True)  109 us
    all_gather x1, waiting for transfers between devices, per_device(): whole_rows = lax.all_gather(normed, 'tp', axis=1, tiled=True)  95.4 us
    dot_general x2, matrix products, gram_product(): lax.dot_general(left, right, (((0,), (0,)), ((), ())), preferred_element_...  15.9 us
  transfers between devices with their start and end apart: 3, of which 2 were waited for; matrix products, arithmetic and copies ran while one was open for 5% of the time, Pallas kernels for 0%

commit v1 on v0

v1 whole, which is shorter than its diff:
```python
import jax
import jax.numpy as jnp
from jax import lax
from jax.sharding import PartitionSpec as P


def gram_product(left, right):
    return lax.dot_general(
        left, right, (((0,), (0,)), ((), ())), preferred_element_type=jnp.float32
    )


def per_device(normed, hidden):
    groups = lax.axis_size("hb")
    scale = 2.0 / (normed.shape[0] * groups)
    swap = [(t * groups + h, h * groups + t) for t in range(groups) for h in range(groups)]
    moved = lax.ppermute(normed, ("tp", "hb"), swap)
    columns = lax.all_gather(moved, "tp", axis=0, tiled=True)
    rows = lax.all_gather(normed, "hb", axis=0, tiled=True)
    units = lax.all_gather(hidden, "hb", axis=0, tiled=True)
    h_in = gram_product(rows, columns) * scale
    width = hidden.shape[1] // groups
    mine = lax.dynamic_slice_in_dim(units, lax.axis_index("hb") * width, width, axis=1)
    h_down = gram_product(mine, units) * scale
    return (h_in, h_down)


def solution(mesh):
    return jax.shard_map(
        per_device,
        mesh=mesh,
        in_specs=(P("hb", "tp"), P("hb", "tp")),
        out_specs=(P("tp", "hb"), P(("tp", "hb"), None)),
        check_vma=False,
    )
```

time: 420 us -> 300 us (0.71)
  blocking collectives: 109 us -> 0 us
  local copies, waits for them, and re-layouts: 8.23 us -> 0.7 us
    unnamed x4 -> x3, waiting for transfers between devices: 172 us -> 1.38 us
    all_gather x2 -> x3, waiting for transfers between devices: 95.4 us -> 266 us  [the longest x1 96.9 us: per_device(): columns = lax.all_gather(moved, 'tp', axis=0, tiled=True)]
    all_to_all x1 -> x0, blocking collectives: 109 us -> none  [per_device(): lax.all_to_all(whole_rows, 'hb', split_axis=1, concat_axis=0, tiled=True)]
    all_to_all x1 -> x0, local copies, waits for them, and re-layouts: 6.38 us -> none  [per_device(): lax.all_to_all(whole_rows, 'hb', split_axis=1, concat_axis=0, tiled=True)]
  transfers between devices with their start and end apart: 3 -> 4, of which waited for: 2 -> 3; matrix products, arithmetic and copies ran while one was open for 5% -> 3% of each run, Pallas kernels for 0% -> 0%
where the time goes in v1:
time: 300 us; the launch traced here: 299 us
  waiting for transfers between devices  267 us (89%)
  matrix products  15.4 us (5%)
  between operations  13.7 us (5%)
    all_gather x1, waiting for transfers between devices, per_device(): columns = lax.all_gather(moved, 'tp', axis=0, tiled=True)  96.9 us
    all_gather x1, waiting for transfers between devices, per_device(): units = lax.all_gather(hidden, 'hb', axis=0, tiled=True)  90 us
    all_gather x1, waiting for transfers between devices, per_device(): rows = lax.all_gather(normed, 'hb', axis=0, tiled=True)  78.9 us
    dot_general x2, matrix products, gram_product(): lax.dot_general(left, right, (((0,), (0,)), ((), ())), preferred_element_...  15.4 us
  transfers between devices with their start and end apart: 4, of which 3 were waited for; matrix products, arithmetic and copies ran while one was open for 3% of the time, Pallas kernels for 0%

profile of v1, /device:TPU:33, one launch (start us, length us, event | category | flops | bytes accessed | tf_op | source)
XLA Modules:
  0.0 298.8 jit_solution(11898271980144473562)
XLA Ops:
  7.2 0.0 all-gather.4.cloned.1.call-start
  7.2 0.7 all-gather.4.cloned.1.call-update
  7.9 0.0 all-gather.6.cloned.1.call-start
  7.9 1.6 collective-permute-start
  9.6 0.0 collective-permute-done
  9.6 0.0 copy-start
  9.6 0.7 copy-done
  10.3 0.0 all-gather.6.cloned.1.call-update
  10.3 0.0 all-gather.8.cloned.1.call-start
  10.3 0.7 all-gather.8.cloned.1.call-update
  11.0 78.9 %all-gather.4.cloned.1.call-done = bf16[2048,1024]{1,0:T(8,128)(2,1)} async-done(((bf16[128,1024]{1,0:T(8,128)(2,1)}), bf16[2048,1024]{1,0:T(8,128)(2,1)}) %all-gather.4.cloned.1.call-update) | async-done | bytes 4194320 | tf_op jit(solution)/shard_map/all_gather | solution.py:19
  89.9 96.9 %all-gather.6.cloned.1.call-done = bf16[2048,1024]{1,0:T(8,128)(2,1)} async-done(((bf16[128,1024]{1,0:T(8,128)(2,1)}), bf16[2048,1024]{1,0:T(8,128)(2,1)}) %all-gather.6.cloned.1.call-update) | async-done | bytes 4194320 | tf_op jit(solution)/shard_map/all_gather | solution.py:18
  186.8 10.0 %convolution_multiply_fusion.1 = f32[1024,1024]{1,0:T(8,128)} fusion(bf16[2048,1024]{1,0:T(8,128)(2,1)} %all-gather.4.cloned.1.call-done, bf16[2048,1024]{1,0:T(8,128)(2,1)} %all-gather.6.cloned.1.call-done), kind=kOutput, calls=%fused_computation.1 | convolution fusion | flops 4296015872 | bytes 12582912 | tf_op jit(solution)/shard_map/dot_general | solution.py:8
  196.9 90.0 %all-gather.8.cloned.1.call-done = bf16[2048,1664]{1,0:T(8,128)(2,1)} async-done(((bf16[128,1664]{1,0:T(8,128)(2,1)}), bf16[2048,1664]{1,0:T(8,128)(2,1)}) %all-gather.8.cloned.1.call-update) | async-done | bytes 6815760 | tf_op jit(solution)/shard_map/all_gather | solution.py:20
  286.9 5.4 %convolution_multiply_fusion = f32[104,1664]{1,0:T(8,128)} fusion(bf16[2048,1664]{1,0:T(8,128)(2,1)} %all-gather.8.cloned.1.call-done, s32[]{:T(128)S(6)} %select_n.3), kind=kOutput, calls=%fused_computation | convolution fusion | flops 709010432 | bytes 8032260 | tf_op jit(solution)/shard_map/dot_general | solution.py:8
Async XLA Ops:
  7.2 82.8 %all-gather.4.cloned.1.call-start = ((), (), s32[]{:S(2)}) async-start(), calls=%async_computation | async-start | bytes 4456448 | tf_op jit(solution)/shard_map/all_gather | solution.py:19
  7.9 178.9 %all-gather.6.cloned.1.call-start = ((), (), s32[]{:S(2)}) async-start(), calls=%async_computation.1 | async-start | bytes 4456448 | tf_op jit(solution)/shard_map/all_gather | solution.py:18
  7.9 1.6 collective-permute-start
  9.6 0.7 copy-start
  10.3 276.6 %all-gather.8.cloned.1.call-start = ((), (), s32[]{:S(2)}) async-start(), calls=%async_computation.2 | async-start | bytes 7241728 | tf_op jit(solution)/shard_map/all_gather | solution.py:20
Sparse Core Ops, SparseCore 0:
  10.7 79.2 all-gather.3
  92.3 94.4 all-gather.5
  189.5 97.3 all-gather.7

commit v2 on v0

v2 whole, which is shorter than its diff:
```python
import functools
import itertools

import jax
import jax.numpy as jnp
from jax import lax
from jax.experimental import pallas as pl
from jax.experimental.pallas import tpu as pltpu
from jax.sharding import PartitionSpec as P

SIZES = (4, 4, 4, 2, 2)
LOOP = (1, 3, 0, 2)
DOT = (((0,), (0,)), ((), ()))
VMEM = pl.BlockSpec(memory_space=pltpu.VMEM)


def linear(place):
    index = 0
    for part, size in zip(place, SIZES):
        index = index * size + part % size
    return index


def send(value, target):
    pairs = [
        (linear(place), linear(target(*place)))
        for place in itertools.product(*map(range, SIZES))
    ]
    return lax.ppermute(value, ("tp", "hb"), pairs)


def up_y(x, zl, y, zh, c):
    return x, zl, y + 1, zh, c


def down_y(x, zl, y, zh, c):
    return x, zl, y - 1, zh, c


def up_x(x, zl, y, zh, c):
    return x + 1, zl, y, zh, c


def down_x(x, zl, y, zh, c):
    return x - 1, zl, y, zh, c


def other_zh(x, zl, y, zh, c):
    return x, zl, y, 1 - zh, c


def other_core(x, zl, y, zh, c):
    return x, zl, y, zh, 1 - c


def next_zl(x, zl, y, zh, c):
    return x, LOOP[zl], y, zh, c


def last_zl(x, zl, y, zh, c):
    return x, LOOP.index(zl), y, zh, c


SPREAD = ((0, 1, 3, 2), (1, 2, 0, 3), (3, 0, 2, 1), (0, 1, 3, 2))
ORIGIN = [0, 0]
for _old, _row in enumerate(SPREAD):
    for _token, _new in enumerate(_row):
        ORIGIN[_old // 2] |= _token << 2 * (_old % 2 * 4 + _new)


def transpose(x, zl, y, zh, c):
    return x + y, SPREAD[zl][zh * 2 + c], x, zl >> 1, zl & 1


class Steps:
    def __init__(self):
        self.last = ()

    def hold(self, *values):
        if self.last:
            values = lax.optimization_barrier((*values, *self.last))[: len(values)]
        return values

    def __call__(self, *moves, slow=0):
        values = self.hold(*(value for value, _ in moves))
        results = [send(value, target) for value, (_, target) in zip(values, moves)]
        self.last = results[slow:]
        return results


def place_of():
    tp, hb = lax.axis_index("tp"), lax.axis_index("hb")
    return tp // 4, tp % 4, hb // 4, hb // 2 % 2, hb % 2


OFFSETS = (0, -1, 1, 2)


def copy_all(pairs, sems):
    copies = [
        pltpu.make_async_copy(source, target, sems.at[k])
        for k, (source, target) in enumerate(pairs)
    ]
    for copy in copies:
        copy.start()
    return copies


def rows_kernel(*refs):
    blocks, panel, sems = refs[:8], refs[8], refs[9]
    _, _, y, zh, _ = place_of()
    pairs = []
    for flip in range(2):
        for offset, block in zip(OFFSETS, blocks[4 * flip : 4 * flip + 4]):
            slot = (y + offset + 4) % 4 * 2 + (zh ^ flip)
            pairs.append((block, panel.at[slot]))
    for copy in copy_all(pairs, sems):
        copy.wait()


def rows_panel(blocks):
    return pl.pallas_call(
        rows_kernel,
        out_shape=jax.ShapeDtypeStruct((8, *blocks[0].shape), blocks[0].dtype),
        in_specs=[VMEM] * 8,
        out_specs=VMEM,
        scratch_shapes=[pltpu.SemaphoreType.DMA((8,))],
        compiler_params=pltpu.CompilerParams(vmem_limit_bytes=4 << 20),
        cost_estimate=pl.CostEstimate(
            flops=0, bytes_accessed=1 << 20, transcendentals=0
        ),
    )(*blocks)


def in_kernel(scale, *refs):
    own, other = refs[:2]
    blocks, out, panel, tiles, sems, out_sems = refs[2:18], *refs[18:]
    x, zl, y, zh, c = place_of()
    codes = jnp.where(zh == 0, ORIGIN[0], ORIGIN[1]) >> 8 * c
    tokens = own.shape[1]
    pairs = []
    for step in range(4):
        for offset, block in zip(OFFSETS, blocks[4 * step : 4 * step + 4]):
            group = codes >> 2 * zl & 3
            slot = (x + offset - y + 8) % 4 * 2 + (group >> 1) + 8 * (group & 1 ^ c)
            at = pl.ds(pl.multiple_of(slot * tokens, tokens), tokens)
            pairs.append((block, panel.at[at, :]))
        zl = jnp.where(zl == 0, 2, jnp.where(zl == 1, 0, jnp.where(zl == 2, 3, 1)))
    for copy in copy_all(pairs, sems):
        copy.wait()
    half, width = 8 * tokens, out.shape[1]
    tile = tiles.shape[1]
    writes = []
    for m in range(out.shape[0] // tile):
        at = slice(m * tile, (m + 1) * tile)
        if m > 1:
            writes[m - 2].wait()
        left = jnp.concatenate(
            [part[:, :, at].reshape(half, tile) for part in (own, other)], axis=0
        )
        tiles[m % 2] = scale * lax.dot_general(
            left, panel[...], DOT, preferred_element_type=jnp.float32
        )
        writes.append(
            pltpu.make_async_copy(tiles.at[m % 2], out.at[at, :], out_sems.at[m % 2])
        )
        writes[-1].start()
    for write in writes[-2:]:
        write.wait()


def in_product(own, other, blocks, scale):
    tokens, width = blocks[0].shape
    count = len(blocks)
    return pl.pallas_call(
        functools.partial(in_kernel, scale),
        out_shape=jax.ShapeDtypeStruct((width, width), jnp.float32),
        in_specs=[VMEM] * (2 + count),
        out_specs=pl.BlockSpec(memory_space=pl.ANY),
        scratch_shapes=[
            pltpu.VMEM((count * tokens, width), jnp.bfloat16),
            pltpu.VMEM((2, width // 4, width), jnp.float32),
            pltpu.SemaphoreType.DMA((count,)),
            pltpu.SemaphoreType.DMA((2,)),
        ],
        compiler_params=pltpu.CompilerParams(vmem_limit_bytes=24 << 20),
        cost_estimate=pl.CostEstimate(
            flops=2 * count * tokens * width * width,
            bytes_accessed=12 << 20,
            transcendentals=0,
        ),
    )(own, other, *blocks)


def down_kernel(scale, *refs):
    blocks, mine, theirs, panel, sems = refs[:8], *refs[8:]
    tokens = blocks[0].shape[0]
    copies = copy_all(
        [(block, panel.at[pl.ds(k * tokens, tokens), :]) for k, block in enumerate(blocks)],
        sems,
    )
    rows, width = mine.shape
    group = lax.axis_index("hb")
    span = 384
    base = jnp.minimum(group // 2 * 2 * rows // 128 * 128, width - span)
    base = pl.multiple_of(base, 128)
    lane = lax.broadcasted_iota(jnp.int32, (span, 256), 1)
    owner = jnp.where(lane < 128, group, group ^ 1)
    wanted = owner * rows - base + (lane & 127)
    pick = lax.broadcasted_iota(jnp.int32, (span, 256), 0) == wanted
    for copy in copies:
        copy.wait()
    left = jnp.dot(
        panel[:, pl.ds(base, span)],
        jnp.where(pick, 1.0, 0.0).astype(jnp.bfloat16),
        preferred_element_type=jnp.float32,
    ).astype(jnp.bfloat16)
    both = scale * lax.dot_general(
        left, panel[...], DOT, preferred_element_type=jnp.float32
    )
    mine[...] = both[:rows]
    theirs[...] = both[128 : 128 + rows]


def down_terms(blocks, scale):
    tokens, width = blocks[0].shape
    rows = width // lax.axis_size("hb")
    term = jax.ShapeDtypeStruct((rows, width), jnp.float32)
    return pl.pallas_call(
        functools.partial(down_kernel, scale),
        out_shape=(term, term),
        in_specs=[VMEM] * 8,
        out_specs=(VMEM, VMEM),
        scratch_shapes=[
            pltpu.VMEM((8 * tokens, width), jnp.bfloat16),
            pltpu.SemaphoreType.DMA((8,)),
        ],
        compiler_params=pltpu.CompilerParams(vmem_limit_bytes=16 << 20),
        cost_estimate=pl.CostEstimate(
            flops=2 * 8 * tokens * 256 * width,
            bytes_accessed=6 << 20,
            transcendentals=0,
        ),
    )(*blocks)


def per_device(normed, hidden):
    scale = 2.0 / (normed.shape[0] * lax.axis_size("hb"))
    step = Steps()
    first, normed_1, n_below, n_above, h_below = step(
        (normed, transpose), (normed, other_zh), (normed, up_y), (normed, down_y), (hidden, up_y)
    )
    second, fourth, x_below_0, x_above_0, h_above = step(
        (first, next_zl), (first, last_zl), (first, up_x), (first, down_x), (hidden, down_y)
    )
    hidden_1, third, x_below_1, x_above_1, n_below_1, n_above_1 = step(
        (hidden, other_zh), (second, next_zl), (second, up_x), (second, down_x),
        (normed_1, up_y), (normed_1, down_y), slow=1,
    )
    x_below_3, x_above_3, x_below_2, x_above_2, n_far, n_far_1 = step(
        (fourth, up_x), (fourth, down_x), (third, up_x), (third, down_x),
        (n_below, up_y), (n_above_1, down_y)
    )
    own = rows_panel(
        [normed, n_below, n_above, n_far, normed_1, n_below_1, n_above_1, n_far_1]
    )
    h_below_1, h_above_1, x_far_0, x_far_1, other = step(
        (hidden_1, up_y), (hidden_1, down_y), (x_below_0, up_x), (x_above_1, down_x),
        (own, other_core)
    )
    h_far_1, h_far, x_far_2, x_far_3 = step(
        (h_above_1, down_y), (h_below, up_y), (x_below_2, up_x), (x_above_3, down_x)
    )
    mine, theirs = down_terms(
        step.hold(hidden, h_below, h_above, h_far, hidden_1, h_below_1, h_above_1, h_far_1),
        scale,
    )
    columns = [
        first, x_below_0, x_above_0, x_far_0,
        second, x_below_1, x_above_1, x_far_1,
        third, x_below_2, x_above_2, x_far_2,
        fourth, x_below_3, x_above_3, x_far_3,
    ]
    h_down = mine + send(theirs, other_core)
    h_in = in_product(own, other, columns, scale)
    return (h_in, h_down)


def solution(mesh):
    return jax.shard_map(
        per_device,
        mesh=mesh,
        in_specs=(P("hb", "tp"), P("hb", "tp")),
        out_specs=(P("tp", "hb"), P(("tp", "hb"), None)),
        check_vma=False,
    )
```

time: 420 us -> 123 us (0.29)
  waiting for transfers between devices: 267 us -> 49.2 us
  blocking collectives: 109 us -> 0 us
  starting transfers between devices: 0.12 us -> 60.3 us
  matrix products: 15.9 us -> 0 us
  between operations: 13.8 us -> 0.72 us
  Pallas kernels: 0 us -> 10.5 us
  local copies, waits for them, and re-layouts: 8.23 us -> 0.95 us
    unnamed x4 -> x0, waiting for transfers between devices: 172 us -> none
    all_to_all x1 -> x0, blocking collectives: 109 us -> none  [per_device(): lax.all_to_all(whole_rows, 'hb', split_axis=1, concat_axis=0, tiled=True)]
    all_gather x2 -> x0, waiting for transfers between devices: 95.4 us -> none  [the longest x1 95.4 us: per_device(): whole_rows = lax.all_gather(normed, 'tp', axis=1, tiled=True)]
    ppermute x0 -> x32, starting transfers between devices: none -> 60.3 us  [send(): return lax.ppermute(value, ('tp', 'hb'), pairs)]
    ppermute x0 -> x32, waiting for transfers between devices: none -> 49.2 us  [send(): return lax.ppermute(value, ('tp', 'hb'), pairs)]
    dot_general x2 -> x0, matrix products: 15.9 us -> none  [gram_product(): lax.dot_general(left, right, (((0,), (0,)), ((), ())), preferred_element_...]
    pallas_call x0 -> x3, Pallas kernels: none -> 10.5 us  [the longest x1 6.43 us: in_product(): pl.pallas_call(functools.partial(in_kernel, scale), out_shape=jax.ShapeDt...]
    all_to_all x1 -> x0, local copies, waits for them, and re-layouts: 6.38 us -> none  [per_device(): lax.all_to_all(whole_rows, 'hb', split_axis=1, concat_axis=0, tiled=True)]
  transfers between devices with their start and end apart: 3 -> 32, of which waited for: 2 -> 14; matrix products, arithmetic and copies ran while one was open for 5% -> 0% of each run, Pallas kernels for 0% -> 5%
where the time goes in v2:
time: 123 us
  starting transfers between devices  60.3 us (49%)
  waiting for transfers between devices  49.2 us (40%)
  Pallas kernels  10.5 us (9%)
    ppermute x32, starting transfers between devices, send(): return lax.ppermute(value, ('tp', 'hb'), pairs)  60.3 us
    ppermute x32, waiting for transfers between devices, send(): return lax.ppermute(value, ('tp', 'hb'), pairs)  49.2 us
    pallas_call x1, Pallas kernels, in_product(): pl.pallas_call(functools.partial(in_kernel, scale), out_shape=jax.ShapeDt...  6.43 us
    pallas_call x1, Pallas kernels, down_terms(): pl.pallas_call(functools.partial(down_kernel, scale), out_shape=(term, te...  3.83 us
  transfers between devices with their start and end apart: 32, of which 14 were waited for; matrix products, arithmetic and copies ran while one was open for 0% of the time, Pallas kernels for 5%

profile of v2, /device:TPU:33, one launch (start us, length us, event | category | flops | bytes accessed | tf_op | source)
XLA Modules:
  0.0 122.6 jit_solution(18434572962968204948)
XLA Ops:
  0.6 1.4 %collective-permute-start.4 = (bf16[128,1664]{1,0:T(8,128)(2,1)}, bf16[128,1664]{1,0:T(8,128)(2,1)S(1)}, u32[]{:S(2)}, u32[]{:S(2)}) collective-permute-start(bf16[128,1664]{1,0:T(8,128)(2,1)} %refs_0_.2), channel_id=1, source_target_pairs={{0,4},{1,5},{2,6},{3,7},{4,8},{5,9},{6,10},{7,11},{8,12},{9,13},{1... | collective-permute-start | bytes 1277960 | tf_op jit(solution)/shard_map/ppermute | solution.py:29
  2.0 1.3 %collective-permute-start = (bf16[128,1024]{1,0:T(8,128)(2,1)}, bf16[128,1024]{1,0:T(8,128)(2,1)S(1)}, u32[]{:S(2)}, u32[]{:S(2)}) collective-permute-start(bf16[128,1024]{1,0:T(8,128)(2,1)} %refs_0_.1), channel_id=1, source_target_pairs={{0,4},{1,5},{2,6},{3,7},{4,8},{5,9},{6,10},{7,11},{8,12},{9,13},{1... | collective-permute-start | bytes 786440 | tf_op jit(solution)/shard_map/ppermute | solution.py:29
  3.3 6.0 %collective-permute-start.3 = (bf16[128,1024]{1,0:T(8,128)(2,1)}, bf16[128,1024]{1,0:T(8,128)(2,1)S(1)}, u32[]{:S(2)}, u32[]{:S(2)}) collective-permute-start(bf16[128,1024]{1,0:T(8,128)(2,1)} %refs_0_.1), channel_id=1, source_target_pairs={{0,2},{1,3},{2,0},{3,1},{4,6},{5,7},{6,4},{7,5},{8,10},{9,11},{10,... | collective-permute-start | bytes 786440 | tf_op jit(solution)/shard_map/ppermute | solution.py:29
  9.3 1.4 %collective-permute-start.1 = (bf16[128,1024]{1,0:T(8,128)(2,1)}, bf16[128,1024]{1,0:T(8,128)(2,1)S(1)}, u32[]{:S(2)}, u32[]{:S(2)}) collective-permute-start(bf16[128,1024]{1,0:T(8,128)(2,1)} %refs_0_.1), channel_id=1, source_target_pairs={{0,12},{1,13},{2,14},{3,15},{4,0},{5,1},{6,2},{7,3},{8,4},{9,5},{1... | collective-permute-start | bytes 786440 | tf_op jit(solution)/shard_map/ppermute | solution.py:29
  10.7 2.6 %collective-permute-start.2 = (bf16[128,1024]{1,0:T(8,128)(2,1)}, bf16[128,1024]{1,0:T(8,128)(2,1)S(1)}, u32[]{:S(2)}, u32[]{:S(2)}) collective-permute-start(bf16[128,1024]{1,0:T(8,128)(2,1)} %refs_0_.1), channel_id=1, source_target_pairs={{0,0},{1,16},{2,48},{3,32},{4,64},{5,80},{6,112},{7,96},{8,128},{9... | collective-permute-start | bytes 786440 | tf_op jit(solution)/shard_map/ppermute | solution.py:29
  13.3 5.2 %collective-permute-done.refs_1_ = bf16[128,1024]{1,0:T(8,128)(2,1)S(1)} collective-permute-done((bf16[128,1024]{1,0:T(8,128)(2,1)}, bf16[128,1024]{1,0:T(8,128)(2,1)S(1)}, u32[]{:S(2)}, u32[]{:S(2)}) %collective-permute-start) | collective-permute-done | bytes 262176 | tf_op jit(solution)/shard_map/ppermute | solution.py:29
  18.6 0.0 collective-permute-done.3.refs_4_
  18.6 0.0 collective-permute-done.1.refs_2_
  18.6 5.3 %collective-permute-done.2.refs_2_ = bf16[128,1024]{1,0:T(8,128)(2,1)S(1)} collective-permute-done((bf16[128,1024]{1,0:T(8,128)(2,1)}, bf16[128,1024]{1,0:T(8,128)(2,1)S(1)}, u32[]{:S(2)}, u32[]{:S(2)}) %collective-permute-start.2) | collective-permute-done | bytes 262176 | tf_op jit(solution)/shard_map/ppermute | solution.py:29
  23.9 1.4 %collective-permute-start.9 = (bf16[128,1664]{1,0:T(8,128)(2,1)}, bf16[128,1664]{1,0:T(8,128)(2,1)S(1)}, u32[]{:S(2)}, u32[]{:S(2)}) collective-permute-start(bf16[128,1664]{1,0:T(8,128)(2,1)} %refs_0_.2), channel_id=1, source_target_pairs={{0,12},{1,13},{2,14},{3,15},{4,0},{5,1},{6,2},{7,3},{8,4},{9,5},{1... | collective-permute-start | bytes 1277960 | tf_op jit(solution)/shard_map/ppermute | solution.py:29
  25.3 5.1 %collective-permute-start.5 = (bf16[128,1024]{1,0:T(8,128)(2,1)S(1)}, bf16[128,1024]{1,0:T(8,128)(2,1)S(1)}, u32[]{:S(2)}, u32[]{:S(2)}) collective-permute-start(bf16[128,1024]{1,0:T(8,128)(2,1)S(1)} %collective-permute-done.2.refs_2_), channel_id=1, source_target_pairs={{0,32},{1,33},{2,34},{3,35},{4,36},{5,37},{6,38},{7,39},{8,40},{9,... | collective-permute-start | bytes 786440 | tf_op jit(solution)/shard_map/ppermute | solution.py:29
  30.4 1.2 collective-permute-start.7
  31.6 2.4 %collective-permute-start.6 = (bf16[128,1024]{1,0:T(8,128)(2,1)S(1)}, bf16[128,1024]{1,0:T(8,128)(2,1)S(1)}, u32[]{:S(2)}, u32[]{:S(2)}) collective-permute-start(bf16[128,1024]{1,0:T(8,128)(2,1)S(1)} %collective-permute-done.2.refs_2_), channel_id=1, source_target_pairs={{0,16},{1,17},{2,18},{3,19},{4,20},{5,21},{6,22},{7,23},{8,24},{9,... | collective-permute-start | bytes 786440 | tf_op jit(solution)/shard_map/ppermute | solution.py:29
  34.0 1.5 %collective-permute-start.8 = (bf16[128,1024]{1,0:T(8,128)(2,1)S(1)}, bf16[128,1024]{1,0:T(8,128)(2,1)S(1)}, u32[]{:S(2)}, u32[]{:S(2)}) collective-permute-start(bf16[128,1024]{1,0:T(8,128)(2,1)S(1)} %collective-permute-done.2.refs_2_), channel_id=1, source_target_pairs={{0,192},{1,193},{2,194},{3,195},{4,196},{5,197},{6,198},{7,199},{8... | collective-permute-start | bytes 786440 | tf_op jit(solution)/shard_map/ppermute | solution.py:29
  35.5 1.4 %collective-permute-done.5.refs_14_ = bf16[128,1024]{1,0:T(8,128)(2,1)S(1)} collective-permute-done((bf16[128,1024]{1,0:T(8,128)(2,1)S(1)}, bf16[128,1024]{1,0:T(8,128)(2,1)S(1)}, u32[]{:S(2)}, u32[]{:S(2)}) %collective-permute-start.5) | collective-permute-done | bytes 262176 | tf_op jit(solution)/shard_map/ppermute | solution.py:29
  36.9 2.0 %collective-permute-done.7.refs_3_ = bf16[128,1024]{1,0:T(8,128)(2,1)S(1)} collective-permute-done((bf16[128,1024]{1,0:T(8,128)(2,1)S(1)}, bf16[128,1024]{1,0:T(8,128)(2,1)S(1)}, u32[]{:S(2)}, u32[]{:S(2)}) %collective-permute-start.7) | collective-permute-done | bytes 262176 | tf_op jit(solution)/shard_map/ppermute | solution.py:29
  38.9 2.8 %collective-permute-done.6.refs_6_ = bf16[128,1024]{1,0:T(8,128)(2,1)S(1)} collective-permute-done((bf16[128,1024]{1,0:T(8,128)(2,1)S(1)}, bf16[128,1024]{1,0:T(8,128)(2,1)S(1)}, u32[]{:S(2)}, u32[]{:S(2)}) %collective-permute-start.6) | collective-permute-done | bytes 262176 | tf_op jit(solution)/shard_map/ppermute | solution.py:29
  41.7 0.3 collective-permute-start.13
  42.1 5.8 %collective-permute-start.10 = (bf16[128,1024]{1,0:T(8,128)(2,1)S(1)}, bf16[128,1024]{1,0:T(8,128)(2,1)S(1)}, u32[]{:S(2)}, u32[]{:S(2)}) collective-permute-start(bf16[128,1024]{1,0:T(8,128)(2,1)S(1)} %collective-permute-done.6.refs_6_), channel_id=1, source_target_pairs={{0,16},{1,17},{2,18},{3,19},{4,20},{5,21},{6,22},{7,23},{8,24},{9,... | collective-permute-start | bytes 786440 | tf_op jit(solution)/shard_map/ppermute | solution.py:29
  47.9 0.3 collective-permute-start.11
  48.2 1.1 collective-permute-start.14
  49.4 2.1 %collective-permute-done.10.refs_10_ = bf16[128,1024]{1,0:T(8,128)(2,1)S(1)} collective-permute-done((bf16[128,1024]{1,0:T(8,128)(2,1)S(1)}, bf16[128,1024]{1,0:T(8,128)(2,1)S(1)}, u32[]{:S(2)}, u32[]{:S(2)}) %collective-permute-start.10) | collective-permute-done | bytes 262176 | tf_op jit(solution)/shard_map/ppermute | solution.py:29
  51.5 1.9 %collective-permute-done.11.refs_6_ = bf16[128,1024]{1,0:T(8,128)(2,1)S(1)} collective-permute-done((bf16[128,1024]{1,0:T(8,128)(2,1)S(1)}, bf16[128,1024]{1,0:T(8,128)(2,1)S(1)}, u32[]{:S(2)}, u32[]{:S(2)}) %collective-permute-start.11) | collective-permute-done | bytes 262176 | tf_op jit(solution)/shard_map/ppermute | solution.py:29
  53.4 1.2 %collective-permute-done.12.refs_7_ = bf16[128,1024]{1,0:T(8,128)(2,1)S(1)} collective-permute-done((bf16[128,1024]{1,0:T(8,128)(2,1)S(1)}, bf16[128,1024]{1,0:T(8,128)(2,1)S(1)}, u32[]{:S(2)}, u32[]{:S(2)}) %collective-permute-start.12) | collective-permute-done | bytes 262176 | tf_op jit(solution)/shard_map/ppermute | solution.py:29
  54.7 1.2 collective-permute-start.15
  55.8 1.5 %collective-permute-start.16 = (bf16[128,1024]{1,0:T(8,128)(2,1)S(1)}, bf16[128,1024]{1,0:T(8,128)(2,1)S(1)}, u32[]{:S(2)}, u32[]{:S(2)}) collective-permute-start(bf16[128,1024]{1,0:T(8,128)(2,1)S(1)} %collective-permute-done.11.refs_6_), channel_id=1, source_target_pairs={{0,12},{1,13},{2,14},{3,15},{4,0},{5,1},{6,2},{7,3},{8,4},{9,5},{1... | collective-permute-start | bytes 786440 | tf_op jit(solution)/shard_map/ppermute | solution.py:29
  57.3 7.7 %collective-permute-start.17 = (bf16[128,1664]{1,0:T(8,128)(2,1)}, bf16[128,1664]{1,0:T(8,128)(2,1)S(1)}, u32[]{:S(2)}, u32[]{:S(2)}) collective-permute-start(bf16[128,1664]{1,0:T(8,128)(2,1)} %refs_0_.2), channel_id=1, source_target_pairs={{0,2},{1,3},{2,0},{3,1},{4,6},{5,7},{6,4},{7,5},{8,10},{9,11},{10,... | collective-permute-start | bytes 1277960 | tf_op jit(solution)/shard_map/ppermute | solution.py:29
  65.1 2.7 %collective-permute-start.19 = (bf16[128,1024]{1,0:T(8,128)(2,1)S(1)}, bf16[128,1024]{1,0:T(8,128)(2,1)S(1)}, u32[]{:S(2)}, u32[]{:S(2)}) collective-permute-start(bf16[128,1024]{1,0:T(8,128)(2,1)S(1)} %collective-permute-done.5.refs_14_), channel_id=1, source_target_pairs={{0,192},{1,193},{2,194},{3,195},{4,196},{5,197},{6,198},{7,199},{8... | collective-permute-start | bytes 786440 | tf_op jit(solution)/shard_map/ppermute | solution.py:29
  67.8 2.7 %collective-permute-start.21 = (bf16[128,1024]{1,0:T(8,128)(2,1)S(1)}, bf16[128,1024]{1,0:T(8,128)(2,1)S(1)}, u32[]{:S(2)}, u32[]{:S(2)}) collective-permute-start(bf16[128,1024]{1,0:T(8,128)(2,1)S(1)} %collective-permute-done.10.refs_10_), channel_id=1, source_target_pairs={{0,192},{1,193},{2,194},{3,195},{4,196},{5,197},{6,198},{7,199},{8... | collective-permute-start | bytes 786440 | tf_op jit(solution)/shard_map/ppermute | solution.py:29
  70.4 0.9 copy-done.1
  71.4 0.2 shard_map.41.refs_0_
  71.6 13.0 %collective-permute-done.17.refs_4_ = bf16[128,1664]{1,0:T(8,128)(2,1)S(1)} collective-permute-done((bf16[128,1664]{1,0:T(8,128)(2,1)}, bf16[128,1664]{1,0:T(8,128)(2,1)S(1)}, u32[]{:S(2)}, u32[]{:S(2)}) %collective-permute-start.17) | collective-permute-done | bytes 426016 | tf_op jit(solution)/shard_map/ppermute | solution.py:29
  84.7 0.7 collective-permute-start.22
  85.3 0.0 collective-permute-start.25
  85.4 1.5 %collective-permute-start.26 = (bf16[128,1664]{1,0:T(8,128)(2,1)S(1)}, bf16[128,1664]{1,0:T(8,128)(2,1)S(1)}, u32[]{:S(2)}, u32[]{:S(2)}) collective-permute-start(bf16[128,1664]{1,0:T(8,128)(2,1)S(1)} %collective-permute-done.17.refs_4_), channel_id=1, source_target_pairs={{0,4},{1,5},{2,6},{3,7},{4,8},{5,9},{6,10},{7,11},{8,12},{9,13},{1... | collective-permute-start | bytes 1277960 | tf_op jit(solution)/shard_map/ppermute | solution.py:29
  86.8 2.7 %collective-permute-start.24 = (bf16[128,1024]{1,0:T(8,128)(2,1)S(1)}, bf16[128,1024]{1,0:T(8,128)(2,1)S(1)}, u32[]{:S(2)}, u32[]{:S(2)}) collective-permute-start(bf16[128,1024]{1,0:T(8,128)(2,1)S(1)} %collective-permute-done.13.refs_8_), channel_id=1, source_target_pairs={{0,192},{1,193},{2,194},{3,195},{4,196},{5,197},{6,198},{7,199},{8... | collective-permute-start | bytes 786440 | tf_op jit(solution)/shard_map/ppermute | solution.py:29
  89.5 5.8 %collective-permute-done.23.refs_5_ = bf16[128,1024]{1,0:T(8,128)(2,1)S(1)} collective-permute-done((bf16[128,1024]{1,0:T(8,128)(2,1)S(1)}, bf16[128,1024]{1,0:T(8,128)(2,1)S(1)}, u32[]{:S(2)}, u32[]{:S(2)}) %collective-permute-start.23) | collective-permute-done | bytes 262176 | tf_op jit(solution)/shard_map/ppermute | solution.py:29
  95.2 1.5 %collective-permute-done.25.refs_6_ = bf16[128,1664]{1,0:T(8,128)(2,1)S(1)} collective-permute-done((bf16[128,1664]{1,0:T(8,128)(2,1)S(1)}, bf16[128,1664]{1,0:T(8,128)(2,1)S(1)}, u32[]{:S(2)}, u32[]{:S(2)}) %collective-permute-start.25) | collective-permute-done | bytes 426016 | tf_op jit(solution)/shard_map/ppermute | solution.py:29
  96.7 0.9 collective-permute-done.26.refs_5_
  97.6 0.3 collective-permute-start.29
  97.9 2.4 %collective-permute-start.30 = (bf16[128,1664]{1,0:T(8,128)(2,1)S(1)}, bf16[128,1664]{1,0:T(8,128)(2,1)S(1)}, u32[]{:S(2)}, u32[]{:S(2)}) collective-permute-start(bf16[128,1664]{1,0:T(8,128)(2,1)S(1)} %collective-permute-done.25.refs_6_), channel_id=1, source_target_pairs={{0,12},{1,13},{2,14},{3,15},{4,0},{5,1},{6,2},{7,3},{8,4},{9,5},{1... | collective-permute-start | bytes 1277960 | tf_op jit(solution)/shard_map/ppermute | solution.py:29
  100.3 2.7 %collective-permute-start.28 = (bf16[128,1024]{1,0:T(8,128)(2,1)S(1)}, bf16[128,1024]{1,0:T(8,128)(2,1)S(1)}, u32[]{:S(2)}, u32[]{:S(2)}) collective-permute-start(bf16[128,1024]{1,0:T(8,128)(2,1)S(1)} %collective-permute-done.19.refs_16_), channel_id=1, source_target_pairs={{0,192},{1,193},{2,194},{3,195},{4,196},{5,197},{6,198},{7,199},{8... | collective-permute-start | bytes 786440 | tf_op jit(solution)/shard_map/ppermute | solution.py:29
  103.0 4.6 %collective-permute-done.27.refs_13_ = bf16[128,1024]{1,0:T(8,128)(2,1)S(1)} collective-permute-done((bf16[128,1024]{1,0:T(8,128)(2,1)S(1)}, bf16[128,1024]{1,0:T(8,128)(2,1)S(1)}, u32[]{:S(2)}, u32[]{:S(2)}) %collective-permute-start.27) | collective-permute-done | bytes 262176 | tf_op jit(solution)/shard_map/ppermute | solution.py:29
  107.6 1.4 %collective-permute-done.29.refs_3_ = bf16[128,1664]{1,0:T(8,128)(2,1)S(1)} collective-permute-done((bf16[128,1664]{1,0:T(8,128)(2,1)S(1)}, bf16[128,1664]{1,0:T(8,128)(2,1)S(1)}, u32[]{:S(2)}, u32[]{:S(2)}) %collective-permute-start.29) | collective-permute-done | bytes 426016 | tf_op jit(solution)/shard_map/ppermute | solution.py:29
  109.0 3.8 %shard_map.43 = (f32[104,1664]{1,0:T(8,128)S(1)}, f32[104,1664]{1,0:T(8,128)S(1)}) custom-call(bf16[128,1664]{1,0:T(8,128)(2,1)S(1)} %copy-done, bf16[128,1664]{1,0:T(8,128)(2,1)S(1)} %collective-permute-done.4.refs_1_, bf16[128,1664]{1,0:T(8,128)(2,1)S(1)} %collective-permute-done.9.refs_2_, bf16[128,1664]{1,0:T(8,128)(2,1)S(1)} %collective-permute-done.29.refs_3_, ...), custom_call_target="tpu_custom_call" | custom-call | flops 872415232 | bytes 6291456 | tf_op jit(solution)/shard_map/pallas_call | solution.py:229
  112.8 2.4 %collective-permute-start.31 = (f32[104,1664]{1,0:T(8,128)S(1)}, f32[104,1664]{1,0:T(8,128)S(1)}, u32[]{:S(2)}, u32[]{:S(2)}) collective-permute-start(f32[104,1664]{1,0:T(8,128)S(1)} %get-tuple-element.73), channel_id=1, source_target_pairs={{0,1},{1,0},{2,3},{3,2},{4,5},{5,4},{6,7},{7,6},{8,9},{9,8},{10,11... | collective-permute-start | bytes 2076680 | tf_op jit(solution)/shard_map/ppermute | solution.py:29
  115.2 6.4 %shard_map.42 = f32[1024,1024]{1,0:T(8,128)} custom-call(bf16[8,128,1024]{2,1,0:T(8,128)(2,1)S(1)} %shard_map.41.refs_0_, bf16[8,128,1024]{2,1,0:T(8,128)(2,1)S(1)} %collective-permute-done.22.refs_1_, bf16[128,1024]{1,0:T(8,128)(2,1)S(1)} %collective-permute-done.2.refs_2_, bf16[128,1024]{1,0:T(8,128)(2,1)S(1)} %collective-permute-done.7.refs_3_, ...), custom_call_target="tpu_custom_call" | custom-call | flops 4294967296 | bytes 12582912 | tf_op jit(solution)/shard_map/pallas_call | solution.py:175
  121.7 0.9 add.3
  (24 shorter events, 0.1 us)
Async XLA Ops:
  0.6 108.3 %copy-start = (bf16[128,1664]{1,0:T(8,128)(2,1)S(1)}, bf16[128,1664]{1,0:T(8,128)(2,1)}, u32[]{:S(2)}) copy-start(bf16[128,1664]{1,0:T(8,128)(2,1)} %refs_0_.2) | copy-start | bytes 1277956
  0.6 23.3 %collective-permute-start.4 = (bf16[128,1664]{1,0:T(8,128)(2,1)}, bf16[128,1664]{1,0:T(8,128)(2,1)S(1)}, u32[]{:S(2)}, u32[]{:S(2)}) collective-permute-start(bf16[128,1664]{1,0:T(8,128)(2,1)} %refs_0_.2), channel_id=1, source_target_pairs={{0,4},{1,5},{2,6},{3,7},{4,8},{5,9},{6,10},{7,11},{8,12},{9,13},{1... | collective-permute-start | bytes 1277960 | tf_op jit(solution)/shard_map/ppermute | solution.py:29
  2.0 16.6 %collective-permute-start = (bf16[128,1024]{1,0:T(8,128)(2,1)}, bf16[128,1024]{1,0:T(8,128)(2,1)S(1)}, u32[]{:S(2)}, u32[]{:S(2)}) collective-permute-start(bf16[128,1024]{1,0:T(8,128)(2,1)} %refs_0_.1), channel_id=1, source_target_pairs={{0,4},{1,5},{2,6},{3,7},{4,8},{5,9},{6,10},{7,11},{8,12},{9,13},{1... | collective-permute-start | bytes 786440 | tf_op jit(solution)/shard_map/ppermute | solution.py:29
  3.3 15.3 %collective-permute-start.3 = (bf16[128,1024]{1,0:T(8,128)(2,1)}, bf16[128,1024]{1,0:T(8,128)(2,1)S(1)}, u32[]{:S(2)}, u32[]{:S(2)}) collective-permute-start(bf16[128,1024]{1,0:T(8,128)(2,1)} %refs_0_.1), channel_id=1, source_target_pairs={{0,2},{1,3},{2,0},{3,1},{4,6},{5,7},{6,4},{7,5},{8,10},{9,11},{10,... | collective-permute-start | bytes 786440 | tf_op jit(solution)/shard_map/ppermute | solution.py:29
  9.3 9.3 %collective-permute-start.1 = (bf16[128,1024]{1,0:T(8,128)(2,1)}, bf16[128,1024]{1,0:T(8,128)(2,1)S(1)}, u32[]{:S(2)}, u32[]{:S(2)}) collective-permute-start(bf16[128,1024]{1,0:T(8,128)(2,1)} %refs_0_.1), channel_id=1, source_target_pairs={{0,12},{1,13},{2,14},{3,15},{4,0},{5,1},{6,2},{7,3},{8,4},{9,5},{1... | collective-permute-start | bytes 786440 | tf_op jit(solution)/shard_map/ppermute | solution.py:29
  10.7 13.2 %collective-permute-start.2 = (bf16[128,1024]{1,0:T(8,128)(2,1)}, bf16[128,1024]{1,0:T(8,128)(2,1)S(1)}, u32[]{:S(2)}, u32[]{:S(2)}) collective-permute-start(bf16[128,1024]{1,0:T(8,128)(2,1)} %refs_0_.1), channel_id=1, source_target_pairs={{0,0},{1,16},{2,48},{3,32},{4,64},{5,80},{6,112},{7,96},{8,128},{9... | collective-permute-start | bytes 786440 | tf_op jit(solution)/shard_map/ppermute | solution.py:29
  23.9 17.8 %collective-permute-start.9 = (bf16[128,1664]{1,0:T(8,128)(2,1)}, bf16[128,1664]{1,0:T(8,128)(2,1)S(1)}, u32[]{:S(2)}, u32[]{:S(2)}) collective-permute-start(bf16[128,1664]{1,0:T(8,128)(2,1)} %refs_0_.2), channel_id=1, source_target_pairs={{0,12},{1,13},{2,14},{3,15},{4,0},{5,1},{6,2},{7,3},{8,4},{9,5},{1... | collective-permute-start | bytes 1277960 | tf_op jit(solution)/shard_map/ppermute | solution.py:29
  25.3 11.5 %collective-permute-start.5 = (bf16[128,1024]{1,0:T(8,128)(2,1)S(1)}, bf16[128,1024]{1,0:T(8,128)(2,1)S(1)}, u32[]{:S(2)}, u32[]{:S(2)}) collective-permute-start(bf16[128,1024]{1,0:T(8,128)(2,1)S(1)} %collective-permute-done.2.refs_2_), channel_id=1, source_target_pairs={{0,32},{1,33},{2,34},{3,35},{4,36},{5,37},{6,38},{7,39},{8,40},{9,... | collective-permute-start | bytes 786440 | tf_op jit(solution)/shard_map/ppermute | solution.py:29
  30.4 8.4 %collective-permute-start.7 = (bf16[128,1024]{1,0:T(8,128)(2,1)S(1)}, bf16[128,1024]{1,0:T(8,128)(2,1)S(1)}, u32[]{:S(2)}, u32[]{:S(2)}) collective-permute-start(bf16[128,1024]{1,0:T(8,128)(2,1)S(1)} %collective-permute-done.2.refs_2_), channel_id=1, source_target_pairs={{0,64},{1,65},{2,66},{3,67},{4,68},{5,69},{6,70},{7,71},{8,72},{9,... | collective-permute-start | bytes 786440 | tf_op jit(solution)/shard_map/ppermute | solution.py:29
  31.6 10.1 %collective-permute-start.6 = (bf16[128,1024]{1,0:T(8,128)(2,1)S(1)}, bf16[128,1024]{1,0:T(8,128)(2,1)S(1)}, u32[]{:S(2)}, u32[]{:S(2)}) collective-permute-start(bf16[128,1024]{1,0:T(8,128)(2,1)S(1)} %collective-permute-done.2.refs_2_), channel_id=1, source_target_pairs={{0,16},{1,17},{2,18},{3,19},{4,20},{5,21},{6,22},{7,23},{8,24},{9,... | collective-permute-start | bytes 786440 | tf_op jit(solution)/shard_map/ppermute | solution.py:29
  34.0 7.8 %collective-permute-start.8 = (bf16[128,1024]{1,0:T(8,128)(2,1)S(1)}, bf16[128,1024]{1,0:T(8,128)(2,1)S(1)}, u32[]{:S(2)}, u32[]{:S(2)}) collective-permute-start(bf16[128,1024]{1,0:T(8,128)(2,1)S(1)} %collective-permute-done.2.refs_2_), channel_id=1, source_target_pairs={{0,192},{1,193},{2,194},{3,195},{4,196},{5,197},{6,198},{7,199},{8... | collective-permute-start | bytes 786440 | tf_op jit(solution)/shard_map/ppermute | solution.py:29
  41.7 7.6 %collective-permute-start.13 = (bf16[128,1024]{1,0:T(8,128)(2,1)S(1)}, bf16[128,1024]{1,0:T(8,128)(2,1)S(1)}, u32[]{:S(2)}, u32[]{:S(2)}) collective-permute-start(bf16[128,1024]{1,0:T(8,128)(2,1)S(1)} %collective-permute-done.6.refs_6_), channel_id=1, source_target_pairs={{0,192},{1,193},{2,194},{3,195},{4,196},{5,197},{6,198},{7,199},{8... | collective-permute-start | bytes 786440 | tf_op jit(solution)/shard_map/ppermute | solution.py:29
  42.1 9.4 %collective-permute-start.10 = (bf16[128,1024]{1,0:T(8,128)(2,1)S(1)}, bf16[128,1024]{1,0:T(8,128)(2,1)S(1)}, u32[]{:S(2)}, u32[]{:S(2)}) collective-permute-start(bf16[128,1024]{1,0:T(8,128)(2,1)S(1)} %collective-permute-done.6.refs_6_), channel_id=1, source_target_pairs={{0,16},{1,17},{2,18},{3,19},{4,20},{5,21},{6,22},{7,23},{8,24},{9,... | collective-permute-start | bytes 786440 | tf_op jit(solution)/shard_map/ppermute | solution.py:29
  47.9 5.5 %collective-permute-start.11 = (bf16[128,1024]{1,0:T(8,128)(2,1)S(1)}, bf16[128,1024]{1,0:T(8,128)(2,1)S(1)}, u32[]{:S(2)}, u32[]{:S(2)}) collective-permute-start(bf16[128,1024]{1,0:T(8,128)(2,1)S(1)} %collective-permute-done.3.refs_4_), channel_id=1, source_target_pairs={{0,12},{1,13},{2,14},{3,15},{4,0},{5,1},{6,2},{7,3},{8,4},{9,5},{1... | collective-permute-start | bytes 786440 | tf_op jit(solution)/shard_map/ppermute | solution.py:29
  48.2 6.4 %collective-permute-start.12 = (bf16[128,1024]{1,0:T(8,128)(2,1)S(1)}, bf16[128,1024]{1,0:T(8,128)(2,1)S(1)}, u32[]{:S(2)}, u32[]{:S(2)}) collective-permute-start(bf16[128,1024]{1,0:T(8,128)(2,1)S(1)} %collective-permute-done.6.refs_6_), channel_id=1, source_target_pairs={{0,64},{1,65},{2,66},{3,67},{4,68},{5,69},{6,70},{7,71},{8,72},{9,... | collective-permute-start | bytes 786440 | tf_op jit(solution)/shard_map/ppermute | solution.py:29
  48.2 6.4 %collective-permute-start.14 = (bf16[128,1024]{1,0:T(8,128)(2,1)S(1)}, bf16[128,1024]{1,0:T(8,128)(2,1)S(1)}, u32[]{:S(2)}, u32[]{:S(2)}) collective-permute-start(bf16[128,1024]{1,0:T(8,128)(2,1)S(1)} %collective-permute-done.3.refs_4_), channel_id=1, source_target_pairs={{0,4},{1,5},{2,6},{3,7},{4,8},{5,9},{6,10},{7,11},{8,12},{9,13},{1... | collective-permute-start | bytes 786440 | tf_op jit(solution)/shard_map/ppermute | solution.py:29
  54.7 13.1 %collective-permute-start.15 = (bf16[128,1024]{1,0:T(8,128)(2,1)S(1)}, bf16[128,1024]{1,0:T(8,128)(2,1)S(1)}, u32[]{:S(2)}, u32[]{:S(2)}) collective-permute-start(bf16[128,1024]{1,0:T(8,128)(2,1)S(1)} %collective-permute-done.refs_1_), channel_id=1, source_target_pairs={{0,4},{1,5},{2,6},{3,7},{4,8},{5,9},{6,10},{7,11},{8,12},{9,13},{1... | collective-permute-start | bytes 786440 | tf_op jit(solution)/shard_map/ppermute | solution.py:29
  55.8 12.0 %collective-permute-start.16 = (bf16[128,1024]{1,0:T(8,128)(2,1)S(1)}, bf16[128,1024]{1,0:T(8,128)(2,1)S(1)}, u32[]{:S(2)}, u32[]{:S(2)}) collective-permute-start(bf16[128,1024]{1,0:T(8,128)(2,1)S(1)} %collective-permute-done.11.refs_6_), channel_id=1, source_target_pairs={{0,12},{1,13},{2,14},{3,15},{4,0},{5,1},{6,2},{7,3},{8,4},{9,5},{1... | collective-permute-start | bytes 786440 | tf_op jit(solution)/shard_map/ppermute | solution.py:29
  57.3 27.3 %collective-permute-start.17 = (bf16[128,1664]{1,0:T(8,128)(2,1)}, bf16[128,1664]{1,0:T(8,128)(2,1)S(1)}, u32[]{:S(2)}, u32[]{:S(2)}) collective-permute-start(bf16[128,1664]{1,0:T(8,128)(2,1)} %refs_0_.2), channel_id=1, source_target_pairs={{0,2},{1,3},{2,0},{3,1},{4,6},{5,7},{6,4},{7,5},{8,10},{9,11},{10,... | collective-permute-start | bytes 1277960 | tf_op jit(solution)/shard_map/ppermute | solution.py:29
  65.1 19.6 %collective-permute-start.18 = (bf16[128,1024]{1,0:T(8,128)(2,1)S(1)}, bf16[128,1024]{1,0:T(8,128)(2,1)S(1)}, u32[]{:S(2)}, u32[]{:S(2)}) collective-permute-start(bf16[128,1024]{1,0:T(8,128)(2,1)S(1)} %collective-permute-done.5.refs_14_), channel_id=1, source_target_pairs={{0,64},{1,65},{2,66},{3,67},{4,68},{5,69},{6,70},{7,71},{8,72},{9,... | collective-permute-start | bytes 786440 | tf_op jit(solution)/shard_map/ppermute | solution.py:29
  65.1 19.6 %collective-permute-start.19 = (bf16[128,1024]{1,0:T(8,128)(2,1)S(1)}, bf16[128,1024]{1,0:T(8,128)(2,1)S(1)}, u32[]{:S(2)}, u32[]{:S(2)}) collective-permute-start(bf16[128,1024]{1,0:T(8,128)(2,1)S(1)} %collective-permute-done.5.refs_14_), channel_id=1, source_target_pairs={{0,192},{1,193},{2,194},{3,195},{4,196},{5,197},{6,198},{7,199},{8... | collective-permute-start | bytes 786440 | tf_op jit(solution)/shard_map/ppermute | solution.py:29
  67.8 16.9 %collective-permute-start.20 = (bf16[128,1024]{1,0:T(8,128)(2,1)S(1)}, bf16[128,1024]{1,0:T(8,128)(2,1)S(1)}, u32[]{:S(2)}, u32[]{:S(2)}) collective-permute-start(bf16[128,1024]{1,0:T(8,128)(2,1)S(1)} %collective-permute-done.10.refs_10_), channel_id=1, source_target_pairs={{0,64},{1,65},{2,66},{3,67},{4,68},{5,69},{6,70},{7,71},{8,72},{9,... | collective-permute-start | bytes 786440 | tf_op jit(solution)/shard_map/ppermute | solution.py:29
  67.8 16.9 %collective-permute-start.21 = (bf16[128,1024]{1,0:T(8,128)(2,1)S(1)}, bf16[128,1024]{1,0:T(8,128)(2,1)S(1)}, u32[]{:S(2)}, u32[]{:S(2)}) collective-permute-start(bf16[128,1024]{1,0:T(8,128)(2,1)S(1)} %collective-permute-done.10.refs_10_), channel_id=1, source_target_pairs={{0,192},{1,193},{2,194},{3,195},{4,196},{5,197},{6,198},{7,199},{8... | collective-permute-start | bytes 786440 | tf_op jit(solution)/shard_map/ppermute | solution.py:29
  70.4 0.9 copy-start.1
  84.7 13.0 %collective-permute-start.22 = (bf16[8,128,1024]{2,1,0:T(8,128)(2,1)S(1)}, bf16[8,128,1024]{2,1,0:T(8,128)(2,1)S(1)}, u32[]{:S(2)}, u32[]{:S(2)}) collective-permute-start(bf16[8,128,1024]{2,1,0:T(8,128)(2,1)S(1)} %shard_map.41.refs_0_), channel_id=1, source_target_pairs={{0,1},{1,0},{2,3},{3,2},{4,5},{5,4},{6,7},{7,6},{8,9},{9,8},{10,11... | collective-permute-start | bytes 6291464 | tf_op jit(solution)/shard_map/ppermute | solution.py:29
  85.3 11.4 %collective-permute-start.25 = (bf16[128,1664]{1,0:T(8,128)(2,1)S(1)}, bf16[128,1664]{1,0:T(8,128)(2,1)S(1)}, u32[]{:S(2)}, u32[]{:S(2)}) collective-permute-start(bf16[128,1664]{1,0:T(8,128)(2,1)S(1)} %collective-permute-done.17.refs_4_), channel_id=1, source_target_pairs={{0,12},{1,13},{2,14},{3,15},{4,0},{5,1},{6,2},{7,3},{8,4},{9,5},{1... | collective-permute-start | bytes 1277960 | tf_op jit(solution)/shard_map/ppermute | solution.py:29
  85.4 12.3 %collective-permute-start.26 = (bf16[128,1664]{1,0:T(8,128)(2,1)S(1)}, bf16[128,1664]{1,0:T(8,128)(2,1)S(1)}, u32[]{:S(2)}, u32[]{:S(2)}) collective-permute-start(bf16[128,1664]{1,0:T(8,128)(2,1)S(1)} %collective-permute-done.17.refs_4_), channel_id=1, source_target_pairs={{0,4},{1,5},{2,6},{3,7},{4,8},{5,9},{6,10},{7,11},{8,12},{9,13},{1... | collective-permute-start | bytes 1277960 | tf_op jit(solution)/shard_map/ppermute | solution.py:29
  86.8 8.4 %collective-permute-start.23 = (bf16[128,1024]{1,0:T(8,128)(2,1)S(1)}, bf16[128,1024]{1,0:T(8,128)(2,1)S(1)}, u32[]{:S(2)}, u32[]{:S(2)}) collective-permute-start(bf16[128,1024]{1,0:T(8,128)(2,1)S(1)} %collective-permute-done.7.refs_3_), channel_id=1, source_target_pairs={{0,64},{1,65},{2,66},{3,67},{4,68},{5,69},{6,70},{7,71},{8,72},{9,... | collective-permute-start | bytes 786440 | tf_op jit(solution)/shard_map/ppermute | solution.py:29
  86.8 8.4 %collective-permute-start.24 = (bf16[128,1024]{1,0:T(8,128)(2,1)S(1)}, bf16[128,1024]{1,0:T(8,128)(2,1)S(1)}, u32[]{:S(2)}, u32[]{:S(2)}) collective-permute-start(bf16[128,1024]{1,0:T(8,128)(2,1)S(1)} %collective-permute-done.13.refs_8_), channel_id=1, source_target_pairs={{0,192},{1,193},{2,194},{3,195},{4,196},{5,197},{6,198},{7,199},{8... | collective-permute-start | bytes 786440 | tf_op jit(solution)/shard_map/ppermute | solution.py:29
  97.6 11.3 %collective-permute-start.29 = (bf16[128,1664]{1,0:T(8,128)(2,1)S(1)}, bf16[128,1664]{1,0:T(8,128)(2,1)S(1)}, u32[]{:S(2)}, u32[]{:S(2)}) collective-permute-start(bf16[128,1664]{1,0:T(8,128)(2,1)S(1)} %collective-permute-done.4.refs_1_), channel_id=1, source_target_pairs={{0,4},{1,5},{2,6},{3,7},{4,8},{5,9},{6,10},{7,11},{8,12},{9,13},{1... | collective-permute-start | bytes 1277960 | tf_op jit(solution)/shard_map/ppermute | solution.py:29
  97.9 11.1 %collective-permute-start.30 = (bf16[128,1664]{1,0:T(8,128)(2,1)S(1)}, bf16[128,1664]{1,0:T(8,128)(2,1)S(1)}, u32[]{:S(2)}, u32[]{:S(2)}) collective-permute-start(bf16[128,1664]{1,0:T(8,128)(2,1)S(1)} %collective-permute-done.25.refs_6_), channel_id=1, source_target_pairs={{0,12},{1,13},{2,14},{3,15},{4,0},{5,1},{6,2},{7,3},{8,4},{9,5},{1... | collective-permute-start | bytes 1277960 | tf_op jit(solution)/shard_map/ppermute | solution.py:29
  100.3 7.3 %collective-permute-start.27 = (bf16[128,1024]{1,0:T(8,128)(2,1)S(1)}, bf16[128,1024]{1,0:T(8,128)(2,1)S(1)}, u32[]{:S(2)}, u32[]{:S(2)}) collective-permute-start(bf16[128,1024]{1,0:T(8,128)(2,1)S(1)} %collective-permute-done.20.refs_11_), channel_id=1, source_target_pairs={{0,64},{1,65},{2,66},{3,67},{4,68},{5,69},{6,70},{7,71},{8,72},{9,... | collective-permute-start | bytes 786440 | tf_op jit(solution)/shard_map/ppermute | solution.py:29
  100.3 7.3 %collective-permute-start.28 = (bf16[128,1024]{1,0:T(8,128)(2,1)S(1)}, bf16[128,1024]{1,0:T(8,128)(2,1)S(1)}, u32[]{:S(2)}, u32[]{:S(2)}) collective-permute-start(bf16[128,1024]{1,0:T(8,128)(2,1)S(1)} %collective-permute-done.19.refs_16_), channel_id=1, source_target_pairs={{0,192},{1,193},{2,194},{3,195},{4,196},{5,197},{6,198},{7,199},{8... | collective-permute-start | bytes 786440 | tf_op jit(solution)/shard_map/ppermute | solution.py:29
  112.8 8.9 %collective-permute-start.31 = (f32[104,1664]{1,0:T(8,128)S(1)}, f32[104,1664]{1,0:T(8,128)S(1)}, u32[]{:S(2)}, u32[]{:S(2)}) collective-permute-start(f32[104,1664]{1,0:T(8,128)S(1)} %get-tuple-element.73), channel_id=1, source_target_pairs={{0,1},{1,0},{2,3},{3,2},{4,5},{5,4},{6,7},{7,6},{8,9},{9,8},{10,11... | collective-permute-start | bytes 2076680 | tf_op jit(solution)/shard_map/ppermute | solution.py:29

commit v3 on v2

--- a/solution.py
+++ b/solution.py
@@ -122,7 +122,7 @@
     return pl.pallas_call(
         rows_kernel,
         out_shape=jax.ShapeDtypeStruct((8, *blocks[0].shape), blocks[0].dtype),
-        in_specs=[VMEM] * 8,
+        in_specs=[pl.BlockSpec(memory_space=pl.ANY)] + [VMEM] * 7,
         out_specs=VMEM,
         scratch_shapes=[pltpu.SemaphoreType.DMA((8,))],
         compiler_params=pltpu.CompilerParams(vmem_limit_bytes=4 << 20),
@@ -132,35 +132,47 @@
     )(*blocks)
 
 
-def in_kernel(scale, *refs):
+def in_kernel(steps, scale, *refs):
     own, other = refs[:2]
-    blocks, out, panel, tiles, sems, out_sems = refs[2:18], *refs[18:]
+    blocks = refs[2 : 2 + 4 * len(steps)]
+    left, right, tiles, sems, out_sems = refs[-5:]
+    out, before = refs[-6], refs[2 + 4 * len(steps) : -6]
     x, zl, y, zh, c = place_of()
     codes = jnp.where(zh == 0, ORIGIN[0], ORIGIN[1]) >> 8 * c
     tokens = own.shape[1]
-    pairs = []
+    copies = []
     for step in range(4):
-        for offset, block in zip(OFFSETS, blocks[4 * step : 4 * step + 4]):
-            group = codes >> 2 * zl & 3
-            slot = (x + offset - y + 8) % 4 * 2 + (group >> 1) + 8 * (group & 1 ^ c)
-            at = pl.ds(pl.multiple_of(slot * tokens, tokens), tokens)
-            pairs.append((block, panel.at[at, :]))
+        group = codes >> 2 * zl & 3
+        swap = group & 1 ^ c
+        for k, offset in enumerate(OFFSETS if step in steps else ()):
+            at = 4 * steps.index(step) + k
+            rows = pl.ds(at * tokens, tokens)
+            slot = (x + offset - y + 8) % 4 * 2 + (group >> 1)
+            copies.append(
+                pltpu.make_async_copy(blocks[at], right.at[rows, :], sems.at[0, at])
+            )
+            copies[-1].start()
+            near = pltpu.make_async_copy(own.at[slot], left.at[rows, :], sems.at[1, at])
+            far = pltpu.make_async_copy(other.at[slot], left.at[rows, :], sems.at[1, at])
+            pl.when(swap == 0)(near.start)
+            pl.when(swap == 1)(far.start)
+            copies.append(near)
         zl = jnp.where(zl == 0, 2, jnp.where(zl == 1, 0, jnp.where(zl == 2, 3, 1)))
-    for copy in copy_all(pairs, sems):
+    for copy in copies:
         copy.wait()
-    half, width = 8 * tokens, out.shape[1]
     tile = tiles.shape[1]
     writes = []
     for m in range(out.shape[0] // tile):
         at = slice(m * tile, (m + 1) * tile)
+        part = scale * lax.dot_general(
+            left[:, at], right[...], DOT, preferred_element_type=jnp.float32
+        )
+        if not before:
+            out[at, :] = part
+            continue
         if m > 1:
             writes[m - 2].wait()
-        left = jnp.concatenate(
-            [part[:, :, at].reshape(half, tile) for part in (own, other)], axis=0
-        )
-        tiles[m % 2] = scale * lax.dot_general(
-            left, panel[...], DOT, preferred_element_type=jnp.float32
-        )
+        tiles[m % 2] = before[0][at, :] + part
         writes.append(
             pltpu.make_async_copy(tiles.at[m % 2], out.at[at, :], out_sems.at[m % 2])
         )
@@ -169,36 +181,39 @@
         write.wait()
 
 
-def in_product(own, other, blocks, scale):
+def in_product(own, other, blocks, steps, scale, before=()):
     tokens, width = blocks[0].shape
     count = len(blocks)
     return pl.pallas_call(
-        functools.partial(in_kernel, scale),
+        functools.partial(in_kernel, steps, scale),
         out_shape=jax.ShapeDtypeStruct((width, width), jnp.float32),
-        in_specs=[VMEM] * (2 + count),
-        out_specs=pl.BlockSpec(memory_space=pl.ANY),
+        in_specs=[VMEM] * (2 + count + len(before)),
+        out_specs=pl.BlockSpec(memory_space=pl.ANY) if before else VMEM,
         scratch_shapes=[
             pltpu.VMEM((count * tokens, width), jnp.bfloat16),
+            pltpu.VMEM((count * tokens, width), jnp.bfloat16),
             pltpu.VMEM((2, width // 4, width), jnp.float32),
-            pltpu.SemaphoreType.DMA((count,)),
+            pltpu.SemaphoreType.DMA((2, count)),
             pltpu.SemaphoreType.DMA((2,)),
         ],
-        compiler_params=pltpu.CompilerParams(vmem_limit_bytes=24 << 20),
+        compiler_params=pltpu.CompilerParams(vmem_limit_bytes=20 << 20),
         cost_estimate=pl.CostEstimate(
             flops=2 * count * tokens * width * width,
-            bytes_accessed=12 << 20,
+            bytes_accessed=8 << 20,
             transcendentals=0,
         ),
-    )(own, other, *blocks)
-
-
-def down_kernel(scale, *refs):
-    blocks, mine, theirs, panel, sems = refs[:8], *refs[8:]
-    tokens = blocks[0].shape[0]
-    copies = copy_all(
-        [(block, panel.at[pl.ds(k * tokens, tokens), :]) for k, block in enumerate(blocks)],
-        sems,
-    )
+    )(own, other, *blocks, *before)
+
+
+def down_kernel(count, scale, *refs):
+    blocks, before = refs[:count], refs[count:-4]
+    mine, theirs, panel, sems = refs[-4:]
+    pairs, start = [], 0
+    for block in blocks:
+        stop = start + block.shape[0]
+        pairs.append((block, panel.at[start:stop, :]))
+        start = stop
+    copies = copy_all(pairs, sems)
     rows, width = mine.shape
     group = lax.axis_index("hb")
     span = 384
@@ -218,40 +233,44 @@
     both = scale * lax.dot_general(
         left, panel[...], DOT, preferred_element_type=jnp.float32
     )
-    mine[...] = both[:rows]
-    theirs[...] = both[128 : 128 + rows]
-
-
-def down_terms(blocks, scale):
-    tokens, width = blocks[0].shape
+    for term, at in ((mine, 0), (theirs, 128)):
+        part = both[at : at + rows]
+        term[...] = part if not before else before[at // 128][...] + part
+
+
+def down_terms(blocks, scale, before=()):
+    width = blocks[0].shape[1]
+    tokens = sum(block.shape[0] for block in blocks)
     rows = width // lax.axis_size("hb")
     term = jax.ShapeDtypeStruct((rows, width), jnp.float32)
+    first = VMEM if before else pl.BlockSpec(memory_space=pl.ANY)
     return pl.pallas_call(
-        functools.partial(down_kernel, scale),
+        functools.partial(down_kernel, len(blocks), scale),
         out_shape=(term, term),
-        in_specs=[VMEM] * 8,
+        in_specs=[first] + [VMEM] * (len(blocks) - 1 + len(before)),
         out_specs=(VMEM, VMEM),
         scratch_shapes=[
-            pltpu.VMEM((8 * tokens, width), jnp.bfloat16),
-            pltpu.SemaphoreType.DMA((8,)),
+            pltpu.VMEM((tokens, width), jnp.bfloat16),
+            pltpu.SemaphoreType.DMA((len(blocks),)),
         ],
         compiler_params=pltpu.CompilerParams(vmem_limit_bytes=16 << 20),
         cost_estimate=pl.CostEstimate(
-            flops=2 * 8 * tokens * 256 * width,
+            flops=2 * tokens * 256 * width,
             bytes_accessed=6 << 20,
             transcendentals=0,
         ),
-    )(*blocks)
+    )(*blocks, *before)
 
 
 def per_device(normed, hidden):
     scale = 2.0 / (normed.shape[0] * lax.axis_size("hb"))
     step = Steps()
-    first, normed_1, n_below, n_above, h_below = step(
-        (normed, transpose), (normed, other_zh), (normed, up_y), (normed, down_y), (hidden, up_y)
-    )
-    second, fourth, x_below_0, x_above_0, h_above = step(
-        (first, next_zl), (first, last_zl), (first, up_x), (first, down_x), (hidden, down_y)
+    first, normed_1, h_below, h_above = step(
+        (normed, transpose), (normed, other_zh), (hidden, up_y), (hidden, down_y)
+    )
+    second, fourth, x_below_0, x_above_0, n_below, n_above = step(
+        (first, next_zl), (first, last_zl), (first, up_x), (first, down_x),
+        (normed, up_y), (normed, down_y)
     )
     hidden_1, third, x_below_1, x_above_1, n_below_1, n_above_1 = step(
         (hidden, other_zh), (second, next_zl), (second, up_x), (second, down_x),
@@ -268,21 +287,19 @@
         (hidden_1, up_y), (hidden_1, down_y), (x_below_0, up_x), (x_above_1, down_x),
         (own, other_core)
     )
+    early = [first, x_below_0, x_above_0, x_far_0, second, x_below_1, x_above_1, x_far_1]
+    partial = in_product(own, other, early, (0, 1), scale)
+    terms = down_terms(
+        [hidden, h_below, h_above, hidden_1, h_below_1, h_above_1], scale
+    )
     h_far_1, h_far, x_far_2, x_far_3 = step(
         (h_above_1, down_y), (h_below, up_y), (x_below_2, up_x), (x_above_3, down_x)
     )
-    mine, theirs = down_terms(
-        step.hold(hidden, h_below, h_above, h_far, hidden_1, h_below_1, h_above_1, h_far_1),
-        scale,
-    )
-    columns = [
-        first, x_below_0, x_above_0, x_far_0,
-        second, x_below_1, x_above_1, x_far_1,
-        third, x_below_2, x_above_2, x_far_2,
-        fourth, x_below_3, x_above_3, x_far_3,
-    ]
+    *held, partial = step.hold(h_far, h_far_1, partial)
+    mine, theirs = down_terms(held, scale, terms)
     h_down = mine + send(theirs, other_core)
-    h_in = in_product(own, other, columns, scale)
+    late = [third, x_below_2, x_above_2, x_far_2, fourth, x_below_3, x_above_3, x_far_3]
+    h_in = in_product(own, other, late, (2, 3), scale, (partial,))
     return (h_in, h_down)
 
 

time: 123 us -> 118 us (0.959)
  waiting for transfers between devices: 49.2 us -> 42.5 us
  Pallas kernels: 10.5 us -> 12.1 us
    ppermute x32, waiting for transfers between devices: 49.2 us -> 42.5 us  [send(): return lax.ppermute(value, ('tp', 'hb'), pairs)]
    pallas_call x2 -> x4, Pallas kernels: 10.3 us -> 11.9 us  [the longest x2 7.66 us: in_product(): pl.pallas_call(functools.partial(in_kernel, steps, scale), out_shape=jax....]
  transfers between devices with their start and end apart: 32 -> 32, of which waited for: 14 -> 12; matrix products, arithmetic and copies ran while one was open for 0% -> 0% of each run, Pallas kernels for 5% -> 9%
where the time goes in v3:
time: 118 us
  starting transfers between devices  60.3 us (51%)
  waiting for transfers between devices  42.5 us (36%)
  Pallas kernels  12.1 us (10%)
    ppermute x32, starting transfers between devices, send(): return lax.ppermute(value, ('tp', 'hb'), pairs)  60.3 us
    ppermute x32, waiting for transfers between devices, send(): return lax.ppermute(value, ('tp', 'hb'), pairs)  42.5 us
    pallas_call x2, Pallas kernels, in_product(): pl.pallas_call(functools.partial(in_kernel, steps, scale), out_shape=jax....  7.66 us
    pallas_call x2, Pallas kernels, down_terms(): pl.pallas_call(functools.partial(down_kernel, len(blocks), scale), out_sh...  4.24 us
  transfers between devices with their start and end apart: 32, of which 12 were waited for; matrix products, arithmetic and copies ran while one was open for 0% of the time, Pallas kernels for 9%

profile of v3, /device:TPU:33, one launch (start us, length us, event | category | flops | bytes accessed | tf_op | source)
XLA Modules:
  0.0 117.6 jit_solution(7128469546418052089)
XLA Ops:
  0.6 1.4 %collective-permute-start.2 = (bf16[128,1664]{1,0:T(8,128)(2,1)}, bf16[128,1664]{1,0:T(8,128)(2,1)S(1)}, u32[]{:S(2)}, u32[]{:S(2)}) collective-permute-start(bf16[128,1664]{1,0:T(8,128)(2,1)} %refs_0_.3), channel_id=1, source_target_pairs={{0,4},{1,5},{2,6},{3,7},{4,8},{5,9},{6,10},{7,11},{8,12},{9,13},{1... | collective-permute-start | bytes 1277960 | tf_op jit(solution)/shard_map/ppermute | solution.py:29
  2.0 1.5 %collective-permute-start.3 = (bf16[128,1664]{1,0:T(8,128)(2,1)}, bf16[128,1664]{1,0:T(8,128)(2,1)S(1)}, u32[]{:S(2)}, u32[]{:S(2)}) collective-permute-start(bf16[128,1664]{1,0:T(8,128)(2,1)} %refs_0_.3), channel_id=1, source_target_pairs={{0,12},{1,13},{2,14},{3,15},{4,0},{5,1},{6,2},{7,3},{8,4},{9,5},{1... | collective-permute-start | bytes 1277960 | tf_op jit(solution)/shard_map/ppermute | solution.py:29
  3.5 6.0 %collective-permute-start.1 = (bf16[128,1024]{1,0:T(8,128)(2,1)}, bf16[128,1024]{1,0:T(8,128)(2,1)S(1)}, u32[]{:S(2)}, u32[]{:S(2)}) collective-permute-start(bf16[128,1024]{1,0:T(8,128)(2,1)} %refs_0_.2), channel_id=1, source_target_pairs={{0,2},{1,3},{2,0},{3,1},{4,6},{5,7},{6,4},{7,5},{8,10},{9,11},{10,... | collective-permute-start | bytes 786440 | tf_op jit(solution)/shard_map/ppermute | solution.py:29
  9.6 2.6 %collective-permute-start = (bf16[128,1024]{1,0:T(8,128)(2,1)}, bf16[128,1024]{1,0:T(8,128)(2,1)S(1)}, u32[]{:S(2)}, u32[]{:S(2)}) collective-permute-start(bf16[128,1024]{1,0:T(8,128)(2,1)} %refs_0_.2), channel_id=1, source_target_pairs={{0,0},{1,16},{2,48},{3,32},{4,64},{5,80},{6,112},{7,96},{8,128},{9... | collective-permute-start | bytes 786440 | tf_op jit(solution)/shard_map/ppermute | solution.py:29
  12.2 7.3 %collective-permute-done.1.refs_4_ = bf16[128,1024]{1,0:T(8,128)(2,1)S(1)} collective-permute-done((bf16[128,1024]{1,0:T(8,128)(2,1)}, bf16[128,1024]{1,0:T(8,128)(2,1)S(1)}, u32[]{:S(2)}, u32[]{:S(2)}) %collective-permute-start.1) | collective-permute-done | bytes 262176 | tf_op jit(solution)/shard_map/ppermute | solution.py:29
  19.5 2.9 %collective-permute-done.refs_2_ = bf16[128,1024]{1,0:T(8,128)(2,1)S(1)} collective-permute-done((bf16[128,1024]{1,0:T(8,128)(2,1)}, bf16[128,1024]{1,0:T(8,128)(2,1)S(1)}, u32[]{:S(2)}, u32[]{:S(2)}) %collective-permute-start) | collective-permute-done | bytes 262176 | tf_op jit(solution)/shard_map/ppermute | solution.py:29
  22.4 1.7 %collective-permute-start.4 = (bf16[128,1024]{1,0:T(8,128)(2,1)}, bf16[128,1024]{1,0:T(8,128)(2,1)S(1)}, u32[]{:S(2)}, u32[]{:S(2)}) collective-permute-start(bf16[128,1024]{1,0:T(8,128)(2,1)} %refs_0_.2), channel_id=1, source_target_pairs={{0,4},{1,5},{2,6},{3,7},{4,8},{5,9},{6,10},{7,11},{8,12},{9,13},{1... | collective-permute-start | bytes 786440 | tf_op jit(solution)/shard_map/ppermute | solution.py:29
  24.1 3.1 %collective-permute-start.6 = (bf16[128,1024]{1,0:T(8,128)(2,1)S(1)}, bf16[128,1024]{1,0:T(8,128)(2,1)S(1)}, u32[]{:S(2)}, u32[]{:S(2)}) collective-permute-start(bf16[128,1024]{1,0:T(8,128)(2,1)S(1)} %collective-permute-done.refs_2_), channel_id=1, source_target_pairs={{0,32},{1,33},{2,34},{3,35},{4,36},{5,37},{6,38},{7,39},{8,40},{9,... | collective-permute-start | bytes 786440 | tf_op jit(solution)/shard_map/ppermute | solution.py:29
  27.2 1.6 %collective-permute-start.8 = (bf16[128,1024]{1,0:T(8,128)(2,1)S(1)}, bf16[128,1024]{1,0:T(8,128)(2,1)S(1)}, u32[]{:S(2)}, u32[]{:S(2)}) collective-permute-start(bf16[128,1024]{1,0:T(8,128)(2,1)S(1)} %collective-permute-done.refs_2_), channel_id=1, source_target_pairs={{0,64},{1,65},{2,66},{3,67},{4,68},{5,69},{6,70},{7,71},{8,72},{9,... | collective-permute-start | bytes 786440 | tf_op jit(solution)/shard_map/ppermute | solution.py:29
  28.8 2.6 %collective-permute-start.5 = (bf16[128,1024]{1,0:T(8,128)(2,1)}, bf16[128,1024]{1,0:T(8,128)(2,1)S(1)}, u32[]{:S(2)}, u32[]{:S(2)}) collective-permute-start(bf16[128,1024]{1,0:T(8,128)(2,1)} %refs_0_.2), channel_id=1, source_target_pairs={{0,12},{1,13},{2,14},{3,15},{4,0},{5,1},{6,2},{7,3},{8,4},{9,5},{1... | collective-permute-start | bytes 786440 | tf_op jit(solution)/shard_map/ppermute | solution.py:29
  31.4 4.0 %collective-permute-start.7 = (bf16[128,1024]{1,0:T(8,128)(2,1)S(1)}, bf16[128,1024]{1,0:T(8,128)(2,1)S(1)}, u32[]{:S(2)}, u32[]{:S(2)}) collective-permute-start(bf16[128,1024]{1,0:T(8,128)(2,1)S(1)} %collective-permute-done.refs_2_), channel_id=1, source_target_pairs={{0,16},{1,17},{2,18},{3,19},{4,20},{5,21},{6,22},{7,23},{8,24},{9,... | collective-permute-start | bytes 786440 | tf_op jit(solution)/shard_map/ppermute | solution.py:29
  35.5 1.5 %collective-permute-start.9 = (bf16[128,1024]{1,0:T(8,128)(2,1)S(1)}, bf16[128,1024]{1,0:T(8,128)(2,1)S(1)}, u32[]{:S(2)}, u32[]{:S(2)}) collective-permute-start(bf16[128,1024]{1,0:T(8,128)(2,1)S(1)} %collective-permute-done.refs_2_), channel_id=1, source_target_pairs={{0,192},{1,193},{2,194},{3,195},{4,196},{5,197},{6,198},{7,199},{8... | collective-permute-start | bytes 786440 | tf_op jit(solution)/shard_map/ppermute | solution.py:29
  36.9 1.3 %collective-permute-done.8.refs_3_ = bf16[128,1024]{1,0:T(8,128)(2,1)S(1)} collective-permute-done((bf16[128,1024]{1,0:T(8,128)(2,1)S(1)}, bf16[128,1024]{1,0:T(8,128)(2,1)S(1)}, u32[]{:S(2)}, u32[]{:S(2)}) %collective-permute-start.8) | collective-permute-done | bytes 262176 | tf_op jit(solution)/shard_map/ppermute | solution.py:29
  38.3 5.9 %collective-permute-done.7.refs_6_ = bf16[128,1024]{1,0:T(8,128)(2,1)S(1)} collective-permute-done((bf16[128,1024]{1,0:T(8,128)(2,1)S(1)}, bf16[128,1024]{1,0:T(8,128)(2,1)S(1)}, u32[]{:S(2)}, u32[]{:S(2)}) %collective-permute-start.7) | collective-permute-done | bytes 262176 | tf_op jit(solution)/shard_map/ppermute | solution.py:29
  44.2 0.2 collective-permute-start.13
  44.4 5.5 %collective-permute-start.10 = (bf16[128,1024]{1,0:T(8,128)(2,1)S(1)}, bf16[128,1024]{1,0:T(8,128)(2,1)S(1)}, u32[]{:S(2)}, u32[]{:S(2)}) collective-permute-start(bf16[128,1024]{1,0:T(8,128)(2,1)S(1)} %collective-permute-done.7.refs_6_), channel_id=1, source_target_pairs={{0,16},{1,17},{2,18},{3,19},{4,20},{5,21},{6,22},{7,23},{8,24},{9,... | collective-permute-start | bytes 786440 | tf_op jit(solution)/shard_map/ppermute | solution.py:29
  49.9 0.1 collective-permute-start.11
  50.0 1.3 %collective-permute-start.14 = (bf16[128,1024]{1,0:T(8,128)(2,1)S(1)}, bf16[128,1024]{1,0:T(8,128)(2,1)S(1)}, u32[]{:S(2)}, u32[]{:S(2)}) collective-permute-start(bf16[128,1024]{1,0:T(8,128)(2,1)S(1)} %collective-permute-done.1.refs_4_), channel_id=1, source_target_pairs={{0,4},{1,5},{2,6},{3,7},{4,8},{5,9},{6,10},{7,11},{8,12},{9,13},{1... | collective-permute-start | bytes 786440 | tf_op jit(solution)/shard_map/ppermute | solution.py:29
  51.4 0.1 collective-permute-done.13.refs_8_
  51.5 1.7 %collective-permute-done.10.refs_2_ = bf16[128,1024]{1,0:T(8,128)(2,1)S(1)} collective-permute-done((bf16[128,1024]{1,0:T(8,128)(2,1)S(1)}, bf16[128,1024]{1,0:T(8,128)(2,1)S(1)}, u32[]{:S(2)}, u32[]{:S(2)}) %collective-permute-start.10) | collective-permute-done | bytes 262176 | tf_op jit(solution)/shard_map/ppermute | solution.py:29
  53.2 1.9 %collective-permute-done.11.refs_6_ = bf16[128,1024]{1,0:T(8,128)(2,1)S(1)} collective-permute-done((bf16[128,1024]{1,0:T(8,128)(2,1)S(1)}, bf16[128,1024]{1,0:T(8,128)(2,1)S(1)}, u32[]{:S(2)}, u32[]{:S(2)}) %collective-permute-start.11) | collective-permute-done | bytes 262176 | tf_op jit(solution)/shard_map/ppermute | solution.py:29
  55.1 1.4 %collective-permute-done.12.refs_7_ = bf16[128,1024]{1,0:T(8,128)(2,1)S(1)} collective-permute-done((bf16[128,1024]{1,0:T(8,128)(2,1)S(1)}, bf16[128,1024]{1,0:T(8,128)(2,1)S(1)}, u32[]{:S(2)}, u32[]{:S(2)}) %collective-permute-start.12) | collective-permute-done | bytes 262176 | tf_op jit(solution)/shard_map/ppermute | solution.py:29
  56.5 1.3 %collective-permute-start.15 = (bf16[128,1024]{1,0:T(8,128)(2,1)S(1)}, bf16[128,1024]{1,0:T(8,128)(2,1)S(1)}, u32[]{:S(2)}, u32[]{:S(2)}) collective-permute-start(bf16[128,1024]{1,0:T(8,128)(2,1)S(1)} %collective-permute-done.4.refs_1_), channel_id=1, source_target_pairs={{0,4},{1,5},{2,6},{3,7},{4,8},{5,9},{6,10},{7,11},{8,12},{9,13},{1... | collective-permute-start | bytes 786440 | tf_op jit(solution)/shard_map/ppermute | solution.py:29
  57.8 1.4 %collective-permute-start.16 = (bf16[128,1024]{1,0:T(8,128)(2,1)S(1)}, bf16[128,1024]{1,0:T(8,128)(2,1)S(1)}, u32[]{:S(2)}, u32[]{:S(2)}) collective-permute-start(bf16[128,1024]{1,0:T(8,128)(2,1)S(1)} %collective-permute-done.11.refs_6_), channel_id=1, source_target_pairs={{0,12},{1,13},{2,14},{3,15},{4,0},{5,1},{6,2},{7,3},{8,4},{9,5},{1... | collective-permute-start | bytes 786440 | tf_op jit(solution)/shard_map/ppermute | solution.py:29
  59.1 5.5 %collective-permute-start.17 = (bf16[128,1664]{1,0:T(8,128)(2,1)}, bf16[128,1664]{1,0:T(8,128)(2,1)S(1)}, u32[]{:S(2)}, u32[]{:S(2)}) collective-permute-start(bf16[128,1664]{1,0:T(8,128)(2,1)} %refs_0_.3), channel_id=1, source_target_pairs={{0,2},{1,3},{2,0},{3,1},{4,6},{5,7},{6,4},{7,5},{8,10},{9,11},{10,... | collective-permute-start | bytes 1277960 | tf_op jit(solution)/shard_map/ppermute | solution.py:29
  64.6 0.5 collective-permute-start.18
  65.1 2.1 %collective-permute-start.19 = (bf16[128,1024]{1,0:T(8,128)(2,1)S(1)}, bf16[128,1024]{1,0:T(8,128)(2,1)S(1)}, u32[]{:S(2)}, u32[]{:S(2)}) collective-permute-start(bf16[128,1024]{1,0:T(8,128)(2,1)S(1)} %collective-permute-done.6.refs_6_), channel_id=1, source_target_pairs={{0,192},{1,193},{2,194},{3,195},{4,196},{5,197},{6,198},{7,199},{8... | collective-permute-start | bytes 786440 | tf_op jit(solution)/shard_map/ppermute | solution.py:29
  67.3 2.7 %collective-permute-start.21 = (bf16[128,1024]{1,0:T(8,128)(2,1)S(1)}, bf16[128,1024]{1,0:T(8,128)(2,1)S(1)}, u32[]{:S(2)}, u32[]{:S(2)}) collective-permute-start(bf16[128,1024]{1,0:T(8,128)(2,1)S(1)} %collective-permute-done.10.refs_2_), channel_id=1, source_target_pairs={{0,192},{1,193},{2,194},{3,195},{4,196},{5,197},{6,198},{7,199},{8... | collective-permute-start | bytes 786440 | tf_op jit(solution)/shard_map/ppermute | solution.py:29
  70.0 0.9 copy-done.1
  70.9 0.2 shard_map.41.refs_0_
  71.1 11.9 %collective-permute-done.17.refs_3_ = bf16[128,1664]{1,0:T(8,128)(2,1)S(1)} collective-permute-done((bf16[128,1664]{1,0:T(8,128)(2,1)}, bf16[128,1664]{1,0:T(8,128)(2,1)S(1)}, u32[]{:S(2)}, u32[]{:S(2)}) %collective-permute-start.17) | collective-permute-done | bytes 426016 | tf_op jit(solution)/shard_map/ppermute | solution.py:29
  83.0 1.5 %collective-permute-start.22 = (bf16[8,128,1024]{2,1,0:T(8,128)(2,1)S(1)}, bf16[8,128,1024]{2,1,0:T(8,128)(2,1)S(1)}, u32[]{:S(2)}, u32[]{:S(2)}) collective-permute-start(bf16[8,128,1024]{2,1,0:T(8,128)(2,1)S(1)} %shard_map.41.refs_0_), channel_id=1, source_target_pairs={{0,1},{1,0},{2,3},{3,2},{4,5},{5,4},{6,7},{7,6},{8,9},{9,8},{10,11... | collective-permute-start | bytes 6291464 | tf_op jit(solution)/shard_map/ppermute | solution.py:29
  84.5 0.2 collective-permute-start.23
  84.7 1.3 %collective-permute-start.24 = (bf16[128,1664]{1,0:T(8,128)(2,1)S(1)}, bf16[128,1664]{1,0:T(8,128)(2,1)S(1)}, u32[]{:S(2)}, u32[]{:S(2)}) collective-permute-start(bf16[128,1664]{1,0:T(8,128)(2,1)S(1)} %collective-permute-done.17.refs_3_), channel_id=1, source_target_pairs={{0,4},{1,5},{2,6},{3,7},{4,8},{5,9},{6,10},{7,11},{8,12},{9,13},{1... | collective-permute-start | bytes 1277960 | tf_op jit(solution)/shard_map/ppermute | solution.py:29
  86.0 0.9 collective-permute-start.25
  86.9 2.0 %collective-permute-start.26 = (bf16[128,1024]{1,0:T(8,128)(2,1)S(1)}, bf16[128,1024]{1,0:T(8,128)(2,1)S(1)}, u32[]{:S(2)}, u32[]{:S(2)}) collective-permute-start(bf16[128,1024]{1,0:T(8,128)(2,1)S(1)} %collective-permute-done.13.refs_8_), channel_id=1, source_target_pairs={{0,192},{1,193},{2,194},{3,195},{4,196},{5,197},{6,198},{7,199},{8... | collective-permute-start | bytes 786440 | tf_op jit(solution)/shard_map/ppermute | solution.py:29
  88.9 6.0 %collective-permute-done.25.refs_5_ = bf16[128,1024]{1,0:T(8,128)(2,1)S(1)} collective-permute-done((bf16[128,1024]{1,0:T(8,128)(2,1)S(1)}, bf16[128,1024]{1,0:T(8,128)(2,1)S(1)}, u32[]{:S(2)}, u32[]{:S(2)}) %collective-permute-start.25) | collective-permute-done | bytes 262176 | tf_op jit(solution)/shard_map/ppermute | solution.py:29
  94.9 1.0 collective-permute-done.23.refs_5_
  95.9 1.1 collective-permute-done.24.refs_4_
  97.0 2.6 %collective-permute-start.30 = (bf16[128,1664]{1,0:T(8,128)(2,1)S(1)}, bf16[128,1664]{1,0:T(8,128)(2,1)S(1)}, u32[]{:S(2)}, u32[]{:S(2)}) collective-permute-start(bf16[128,1664]{1,0:T(8,128)(2,1)S(1)} %collective-permute-done.23.refs_5_), channel_id=1, source_target_pairs={{0,12},{1,13},{2,14},{3,15},{4,0},{5,1},{6,2},{7,3},{8,4},{9,5},{1... | collective-permute-start | bytes 1277960 | tf_op jit(solution)/shard_map/ppermute | solution.py:29
  99.6 0.7 collective-permute-start.27
  100.4 2.0 %collective-permute-start.28 = (bf16[128,1024]{1,0:T(8,128)(2,1)S(1)}, bf16[128,1024]{1,0:T(8,128)(2,1)S(1)}, u32[]{:S(2)}, u32[]{:S(2)}) collective-permute-start(bf16[128,1024]{1,0:T(8,128)(2,1)S(1)} %collective-permute-done.19.refs_8_), channel_id=1, source_target_pairs={{0,192},{1,193},{2,194},{3,195},{4,196},{5,197},{6,198},{7,199},{8... | collective-permute-start | bytes 786440 | tf_op jit(solution)/shard_map/ppermute | solution.py:29
  102.4 3.0 %shard_map.44 = (f32[104,1664]{1,0:T(8,128)S(1)}, f32[104,1664]{1,0:T(8,128)S(1)}) custom-call(bf16[128,1664]{1,0:T(8,128)(2,1)S(1)} %copy-done, bf16[128,1664]{1,0:T(8,128)(2,1)S(1)} %collective-permute-done.2.refs_1_, bf16[128,1664]{1,0:T(8,128)(2,1)S(1)} %collective-permute-done.3.refs_2_, bf16[128,1664]{1,0:T(8,128)(2,1)S(1)} %collective-permute-done.17.refs_3_, ...), custom_call_target="tpu_custom_call" | custom-call | flops 654311424 | bytes 6291456 | tf_op jit(solution)/shard_map/pallas_call | solution.py:247
  105.4 3.2 %shard_map.42.refs_10_ = f32[1024,1024]{1,0:T(8,128)S(1)} custom-call(bf16[8,128,1024]{2,1,0:T(8,128)(2,1)S(1)} %shard_map.41.refs_0_, bf16[8,128,1024]{2,1,0:T(8,128)(2,1)S(1)} %collective-permute-done.22.refs_1_, bf16[128,1024]{1,0:T(8,128)(2,1)S(1)} %collective-permute-done.refs_2_, bf16[128,1024]{1,0:T(8,128)(2,1)S(1)} %collective-permute-done.8.refs_3_, ...), custom_call_target="tpu_custom_call" | custom-call | flops 2147483648 | bytes 8388608 | tf_op jit(solution)/shard_map/pallas_call | solution.py:187
  108.6 1.3 %shard_map.45 = (f32[104,1664]{1,0:T(8,128)S(1)}, f32[104,1664]{1,0:T(8,128)S(1)}) custom-call(bf16[128,1664]{1,0:T(8,128)(2,1)S(1)} %collective-permute-done.29.refs_0_, bf16[128,1664]{1,0:T(8,128)(2,1)S(1)} %collective-permute-done.30.refs_1_, f32[104,1664]{1,0:T(8,128)S(1)} %get-tuple-element.66.refs_2_, f32[104,1664]{1,0:T(8,128)S(1)} %get-tuple-element.67.refs_3_), custom_call_target="tpu_custom_call" | custom-call | flops 218103808 | bytes 6291456 | tf_op jit(solution)/shard_map/pallas_call | solution.py:247
  109.9 2.3 %collective-permute-start.31 = (f32[104,1664]{1,0:T(8,128)S(1)}, f32[104,1664]{1,0:T(8,128)S(1)}, u32[]{:S(2)}, u32[]{:S(2)}) collective-permute-start(f32[104,1664]{1,0:T(8,128)S(1)} %get-tuple-element.69), channel_id=1, source_target_pairs={{0,1},{1,0},{2,3},{3,2},{4,5},{5,4},{6,7},{7,6},{8,9},{9,8},{10,11... | collective-permute-start | bytes 2076680 | tf_op jit(solution)/shard_map/ppermute | solution.py:29
  112.2 4.5 %shard_map.43 = f32[1024,1024]{1,0:T(8,128)} custom-call(bf16[8,128,1024]{2,1,0:T(8,128)(2,1)S(1)} %shard_map.41.refs_0_, bf16[8,128,1024]{2,1,0:T(8,128)(2,1)S(1)} %collective-permute-done.22.refs_1_, bf16[128,1024]{1,0:T(8,128)(2,1)S(1)} %collective-permute-done.10.refs_2_, bf16[128,1024]{1,0:T(8,128)(2,1)S(1)} %collective-permute-done.20.refs_3_, ...), custom_call_target="tpu_custom_call" | custom-call | flops 2147483648 | bytes 8388608 | tf_op jit(solution)/shard_map/pallas_call | solution.py:187
  116.7 0.9 add.3
  (26 shorter events, 0.1 us)
Async XLA Ops:
  0.6 101.7 %copy-start = (bf16[128,1664]{1,0:T(8,128)(2,1)S(1)}, bf16[128,1664]{1,0:T(8,128)(2,1)}, u32[]{:S(2)}) copy-start(bf16[128,1664]{1,0:T(8,128)(2,1)} %refs_0_.3) | copy-start | bytes 1277956
  0.6 21.8 %collective-permute-start.2 = (bf16[128,1664]{1,0:T(8,128)(2,1)}, bf16[128,1664]{1,0:T(8,128)(2,1)S(1)}, u32[]{:S(2)}, u32[]{:S(2)}) collective-permute-start(bf16[128,1664]{1,0:T(8,128)(2,1)} %refs_0_.3), channel_id=1, source_target_pairs={{0,4},{1,5},{2,6},{3,7},{4,8},{5,9},{6,10},{7,11},{8,12},{9,13},{1... | collective-permute-start | bytes 1277960 | tf_op jit(solution)/shard_map/ppermute | solution.py:29
  2.0 20.4 %collective-permute-start.3 = (bf16[128,1664]{1,0:T(8,128)(2,1)}, bf16[128,1664]{1,0:T(8,128)(2,1)S(1)}, u32[]{:S(2)}, u32[]{:S(2)}) collective-permute-start(bf16[128,1664]{1,0:T(8,128)(2,1)} %refs_0_.3), channel_id=1, source_target_pairs={{0,12},{1,13},{2,14},{3,15},{4,0},{5,1},{6,2},{7,3},{8,4},{9,5},{1... | collective-permute-start | bytes 1277960 | tf_op jit(solution)/shard_map/ppermute | solution.py:29
  3.5 15.9 %collective-permute-start.1 = (bf16[128,1024]{1,0:T(8,128)(2,1)}, bf16[128,1024]{1,0:T(8,128)(2,1)S(1)}, u32[]{:S(2)}, u32[]{:S(2)}) collective-permute-start(bf16[128,1024]{1,0:T(8,128)(2,1)} %refs_0_.2), channel_id=1, source_target_pairs={{0,2},{1,3},{2,0},{3,1},{4,6},{5,7},{6,4},{7,5},{8,10},{9,11},{10,... | collective-permute-start | bytes 786440 | tf_op jit(solution)/shard_map/ppermute | solution.py:29
  9.6 12.9 %collective-permute-start = (bf16[128,1024]{1,0:T(8,128)(2,1)}, bf16[128,1024]{1,0:T(8,128)(2,1)S(1)}, u32[]{:S(2)}, u32[]{:S(2)}) collective-permute-start(bf16[128,1024]{1,0:T(8,128)(2,1)} %refs_0_.2), channel_id=1, source_target_pairs={{0,0},{1,16},{2,48},{3,32},{4,64},{5,80},{6,112},{7,96},{8,128},{9... | collective-permute-start | bytes 786440 | tf_op jit(solution)/shard_map/ppermute | solution.py:29
  22.4 13.1 %collective-permute-start.4 = (bf16[128,1024]{1,0:T(8,128)(2,1)}, bf16[128,1024]{1,0:T(8,128)(2,1)S(1)}, u32[]{:S(2)}, u32[]{:S(2)}) collective-permute-start(bf16[128,1024]{1,0:T(8,128)(2,1)} %refs_0_.2), channel_id=1, source_target_pairs={{0,4},{1,5},{2,6},{3,7},{4,8},{5,9},{6,10},{7,11},{8,12},{9,13},{1... | collective-permute-start | bytes 786440 | tf_op jit(solution)/shard_map/ppermute | solution.py:29
  24.1 12.8 %collective-permute-start.6 = (bf16[128,1024]{1,0:T(8,128)(2,1)S(1)}, bf16[128,1024]{1,0:T(8,128)(2,1)S(1)}, u32[]{:S(2)}, u32[]{:S(2)}) collective-permute-start(bf16[128,1024]{1,0:T(8,128)(2,1)S(1)} %collective-permute-done.refs_2_), channel_id=1, source_target_pairs={{0,32},{1,33},{2,34},{3,35},{4,36},{5,37},{6,38},{7,39},{8,40},{9,... | collective-permute-start | bytes 786440 | tf_op jit(solution)/shard_map/ppermute | solution.py:29
  27.2 11.0 %collective-permute-start.8 = (bf16[128,1024]{1,0:T(8,128)(2,1)S(1)}, bf16[128,1024]{1,0:T(8,128)(2,1)S(1)}, u32[]{:S(2)}, u32[]{:S(2)}) collective-permute-start(bf16[128,1024]{1,0:T(8,128)(2,1)S(1)} %collective-permute-done.refs_2_), channel_id=1, source_target_pairs={{0,64},{1,65},{2,66},{3,67},{4,68},{5,69},{6,70},{7,71},{8,72},{9,... | collective-permute-start | bytes 786440 | tf_op jit(solution)/shard_map/ppermute | solution.py:29
  28.8 9.4 %collective-permute-start.5 = (bf16[128,1024]{1,0:T(8,128)(2,1)}, bf16[128,1024]{1,0:T(8,128)(2,1)S(1)}, u32[]{:S(2)}, u32[]{:S(2)}) collective-permute-start(bf16[128,1024]{1,0:T(8,128)(2,1)} %refs_0_.2), channel_id=1, source_target_pairs={{0,12},{1,13},{2,14},{3,15},{4,0},{5,1},{6,2},{7,3},{8,4},{9,5},{1... | collective-permute-start | bytes 786440 | tf_op jit(solution)/shard_map/ppermute | solution.py:29
  31.4 12.8 %collective-permute-start.7 = (bf16[128,1024]{1,0:T(8,128)(2,1)S(1)}, bf16[128,1024]{1,0:T(8,128)(2,1)S(1)}, u32[]{:S(2)}, u32[]{:S(2)}) collective-permute-start(bf16[128,1024]{1,0:T(8,128)(2,1)S(1)} %collective-permute-done.refs_2_), channel_id=1, source_target_pairs={{0,16},{1,17},{2,18},{3,19},{4,20},{5,21},{6,22},{7,23},{8,24},{9,... | collective-permute-start | bytes 786440 | tf_op jit(solution)/shard_map/ppermute | solution.py:29
  35.5 8.7 %collective-permute-start.9 = (bf16[128,1024]{1,0:T(8,128)(2,1)S(1)}, bf16[128,1024]{1,0:T(8,128)(2,1)S(1)}, u32[]{:S(2)}, u32[]{:S(2)}) collective-permute-start(bf16[128,1024]{1,0:T(8,128)(2,1)S(1)} %collective-permute-done.refs_2_), channel_id=1, source_target_pairs={{0,192},{1,193},{2,194},{3,195},{4,196},{5,197},{6,198},{7,199},{8... | collective-permute-start | bytes 786440 | tf_op jit(solution)/shard_map/ppermute | solution.py:29
  44.2 7.3 %collective-permute-start.13 = (bf16[128,1024]{1,0:T(8,128)(2,1)S(1)}, bf16[128,1024]{1,0:T(8,128)(2,1)S(1)}, u32[]{:S(2)}, u32[]{:S(2)}) collective-permute-start(bf16[128,1024]{1,0:T(8,128)(2,1)S(1)} %collective-permute-done.7.refs_6_), channel_id=1, source_target_pairs={{0,192},{1,193},{2,194},{3,195},{4,196},{5,197},{6,198},{7,199},{8... | collective-permute-start | bytes 786440 | tf_op jit(solution)/shard_map/ppermute | solution.py:29
  44.4 8.8 %collective-permute-start.10 = (bf16[128,1024]{1,0:T(8,128)(2,1)S(1)}, bf16[128,1024]{1,0:T(8,128)(2,1)S(1)}, u32[]{:S(2)}, u32[]{:S(2)}) collective-permute-start(bf16[128,1024]{1,0:T(8,128)(2,1)S(1)} %collective-permute-done.7.refs_6_), channel_id=1, source_target_pairs={{0,16},{1,17},{2,18},{3,19},{4,20},{5,21},{6,22},{7,23},{8,24},{9,... | collective-permute-start | bytes 786440 | tf_op jit(solution)/shard_map/ppermute | solution.py:29
  49.9 5.2 %collective-permute-start.11 = (bf16[128,1024]{1,0:T(8,128)(2,1)S(1)}, bf16[128,1024]{1,0:T(8,128)(2,1)S(1)}, u32[]{:S(2)}, u32[]{:S(2)}) collective-permute-start(bf16[128,1024]{1,0:T(8,128)(2,1)S(1)} %collective-permute-done.1.refs_4_), channel_id=1, source_target_pairs={{0,12},{1,13},{2,14},{3,15},{4,0},{5,1},{6,2},{7,3},{8,4},{9,5},{1... | collective-permute-start | bytes 786440 | tf_op jit(solution)/shard_map/ppermute | solution.py:29
  50.0 6.4 %collective-permute-start.12 = (bf16[128,1024]{1,0:T(8,128)(2,1)S(1)}, bf16[128,1024]{1,0:T(8,128)(2,1)S(1)}, u32[]{:S(2)}, u32[]{:S(2)}) collective-permute-start(bf16[128,1024]{1,0:T(8,128)(2,1)S(1)} %collective-permute-done.7.refs_6_), channel_id=1, source_target_pairs={{0,64},{1,65},{2,66},{3,67},{4,68},{5,69},{6,70},{7,71},{8,72},{9,... | collective-permute-start | bytes 786440 | tf_op jit(solution)/shard_map/ppermute | solution.py:29
  50.0 6.4 %collective-permute-start.14 = (bf16[128,1024]{1,0:T(8,128)(2,1)S(1)}, bf16[128,1024]{1,0:T(8,128)(2,1)S(1)}, u32[]{:S(2)}, u32[]{:S(2)}) collective-permute-start(bf16[128,1024]{1,0:T(8,128)(2,1)S(1)} %collective-permute-done.1.refs_4_), channel_id=1, source_target_pairs={{0,4},{1,5},{2,6},{3,7},{4,8},{5,9},{6,10},{7,11},{8,12},{9,13},{1... | collective-permute-start | bytes 786440 | tf_op jit(solution)/shard_map/ppermute | solution.py:29
  56.5 10.8 %collective-permute-start.15 = (bf16[128,1024]{1,0:T(8,128)(2,1)S(1)}, bf16[128,1024]{1,0:T(8,128)(2,1)S(1)}, u32[]{:S(2)}, u32[]{:S(2)}) collective-permute-start(bf16[128,1024]{1,0:T(8,128)(2,1)S(1)} %collective-permute-done.4.refs_1_), channel_id=1, source_target_pairs={{0,4},{1,5},{2,6},{3,7},{4,8},{5,9},{6,10},{7,11},{8,12},{9,13},{1... | collective-permute-start | bytes 786440 | tf_op jit(solution)/shard_map/ppermute | solution.py:29
  57.8 9.5 %collective-permute-start.16 = (bf16[128,1024]{1,0:T(8,128)(2,1)S(1)}, bf16[128,1024]{1,0:T(8,128)(2,1)S(1)}, u32[]{:S(2)}, u32[]{:S(2)}) collective-permute-start(bf16[128,1024]{1,0:T(8,128)(2,1)S(1)} %collective-permute-done.11.refs_6_), channel_id=1, source_target_pairs={{0,12},{1,13},{2,14},{3,15},{4,0},{5,1},{6,2},{7,3},{8,4},{9,5},{1... | collective-permute-start | bytes 786440 | tf_op jit(solution)/shard_map/ppermute | solution.py:29
  59.1 23.9 %collective-permute-start.17 = (bf16[128,1664]{1,0:T(8,128)(2,1)}, bf16[128,1664]{1,0:T(8,128)(2,1)S(1)}, u32[]{:S(2)}, u32[]{:S(2)}) collective-permute-start(bf16[128,1664]{1,0:T(8,128)(2,1)} %refs_0_.3), channel_id=1, source_target_pairs={{0,2},{1,3},{2,0},{3,1},{4,6},{5,7},{6,4},{7,5},{8,10},{9,11},{10,... | collective-permute-start | bytes 1277960 | tf_op jit(solution)/shard_map/ppermute | solution.py:29
  64.6 18.4 %collective-permute-start.18 = (bf16[128,1024]{1,0:T(8,128)(2,1)S(1)}, bf16[128,1024]{1,0:T(8,128)(2,1)S(1)}, u32[]{:S(2)}, u32[]{:S(2)}) collective-permute-start(bf16[128,1024]{1,0:T(8,128)(2,1)S(1)} %collective-permute-done.6.refs_6_), channel_id=1, source_target_pairs={{0,64},{1,65},{2,66},{3,67},{4,68},{5,69},{6,70},{7,71},{8,72},{9,... | collective-permute-start | bytes 786440 | tf_op jit(solution)/shard_map/ppermute | solution.py:29
  65.1 17.9 %collective-permute-start.19 = (bf16[128,1024]{1,0:T(8,128)(2,1)S(1)}, bf16[128,1024]{1,0:T(8,128)(2,1)S(1)}, u32[]{:S(2)}, u32[]{:S(2)}) collective-permute-start(bf16[128,1024]{1,0:T(8,128)(2,1)S(1)} %collective-permute-done.6.refs_6_), channel_id=1, source_target_pairs={{0,192},{1,193},{2,194},{3,195},{4,196},{5,197},{6,198},{7,199},{8... | collective-permute-start | bytes 786440 | tf_op jit(solution)/shard_map/ppermute | solution.py:29
  67.3 15.7 %collective-permute-start.20 = (bf16[128,1024]{1,0:T(8,128)(2,1)S(1)}, bf16[128,1024]{1,0:T(8,128)(2,1)S(1)}, u32[]{:S(2)}, u32[]{:S(2)}) collective-permute-start(bf16[128,1024]{1,0:T(8,128)(2,1)S(1)} %collective-permute-done.10.refs_2_), channel_id=1, source_target_pairs={{0,64},{1,65},{2,66},{3,67},{4,68},{5,69},{6,70},{7,71},{8,72},{9,... | collective-permute-start | bytes 786440 | tf_op jit(solution)/shard_map/ppermute | solution.py:29
  67.3 15.7 %collective-permute-start.21 = (bf16[128,1024]{1,0:T(8,128)(2,1)S(1)}, bf16[128,1024]{1,0:T(8,128)(2,1)S(1)}, u32[]{:S(2)}, u32[]{:S(2)}) collective-permute-start(bf16[128,1024]{1,0:T(8,128)(2,1)S(1)} %collective-permute-done.10.refs_2_), channel_id=1, source_target_pairs={{0,192},{1,193},{2,194},{3,195},{4,196},{5,197},{6,198},{7,199},{8... | collective-permute-start | bytes 786440 | tf_op jit(solution)/shard_map/ppermute | solution.py:29
  70.0 0.9 copy-start.1
  83.0 13.9 %collective-permute-start.22 = (bf16[8,128,1024]{2,1,0:T(8,128)(2,1)S(1)}, bf16[8,128,1024]{2,1,0:T(8,128)(2,1)S(1)}, u32[]{:S(2)}, u32[]{:S(2)}) collective-permute-start(bf16[8,128,1024]{2,1,0:T(8,128)(2,1)S(1)} %shard_map.41.refs_0_), channel_id=1, source_target_pairs={{0,1},{1,0},{2,3},{3,2},{4,5},{5,4},{6,7},{7,6},{8,9},{9,8},{10,11... | collective-permute-start | bytes 6291464 | tf_op jit(solution)/shard_map/ppermute | solution.py:29
  84.5 11.4 %collective-permute-start.23 = (bf16[128,1664]{1,0:T(8,128)(2,1)S(1)}, bf16[128,1664]{1,0:T(8,128)(2,1)S(1)}, u32[]{:S(2)}, u32[]{:S(2)}) collective-permute-start(bf16[128,1664]{1,0:T(8,128)(2,1)S(1)} %collective-permute-done.17.refs_3_), channel_id=1, source_target_pairs={{0,12},{1,13},{2,14},{3,15},{4,0},{5,1},{6,2},{7,3},{8,4},{9,5},{1... | collective-permute-start | bytes 1277960 | tf_op jit(solution)/shard_map/ppermute | solution.py:29
  84.7 12.3 %collective-permute-start.24 = (bf16[128,1664]{1,0:T(8,128)(2,1)S(1)}, bf16[128,1664]{1,0:T(8,128)(2,1)S(1)}, u32[]{:S(2)}, u32[]{:S(2)}) collective-permute-start(bf16[128,1664]{1,0:T(8,128)(2,1)S(1)} %collective-permute-done.17.refs_3_), channel_id=1, source_target_pairs={{0,4},{1,5},{2,6},{3,7},{4,8},{5,9},{6,10},{7,11},{8,12},{9,13},{1... | collective-permute-start | bytes 1277960 | tf_op jit(solution)/shard_map/ppermute | solution.py:29
  86.0 8.9 %collective-permute-start.25 = (bf16[128,1024]{1,0:T(8,128)(2,1)S(1)}, bf16[128,1024]{1,0:T(8,128)(2,1)S(1)}, u32[]{:S(2)}, u32[]{:S(2)}) collective-permute-start(bf16[128,1024]{1,0:T(8,128)(2,1)S(1)} %collective-permute-done.8.refs_3_), channel_id=1, source_target_pairs={{0,64},{1,65},{2,66},{3,67},{4,68},{5,69},{6,70},{7,71},{8,72},{9,... | collective-permute-start | bytes 786440 | tf_op jit(solution)/shard_map/ppermute | solution.py:29
  86.9 8.0 %collective-permute-start.26 = (bf16[128,1024]{1,0:T(8,128)(2,1)S(1)}, bf16[128,1024]{1,0:T(8,128)(2,1)S(1)}, u32[]{:S(2)}, u32[]{:S(2)}) collective-permute-start(bf16[128,1024]{1,0:T(8,128)(2,1)S(1)} %collective-permute-done.13.refs_8_), channel_id=1, source_target_pairs={{0,192},{1,193},{2,194},{3,195},{4,196},{5,197},{6,198},{7,199},{8... | collective-permute-start | bytes 786440 | tf_op jit(solution)/shard_map/ppermute | solution.py:29
  97.0 11.6 %collective-permute-start.29 = (bf16[128,1664]{1,0:T(8,128)(2,1)S(1)}, bf16[128,1664]{1,0:T(8,128)(2,1)S(1)}, u32[]{:S(2)}, u32[]{:S(2)}) collective-permute-start(bf16[128,1664]{1,0:T(8,128)(2,1)S(1)} %collective-permute-done.2.refs_1_), channel_id=1, source_target_pairs={{0,4},{1,5},{2,6},{3,7},{4,8},{5,9},{6,10},{7,11},{8,12},{9,13},{1... | collective-permute-start | bytes 1277960 | tf_op jit(solution)/shard_map/ppermute | solution.py:29
  97.0 11.6 %collective-permute-start.30 = (bf16[128,1664]{1,0:T(8,128)(2,1)S(1)}, bf16[128,1664]{1,0:T(8,128)(2,1)S(1)}, u32[]{:S(2)}, u32[]{:S(2)}) collective-permute-start(bf16[128,1664]{1,0:T(8,128)(2,1)S(1)} %collective-permute-done.23.refs_5_), channel_id=1, source_target_pairs={{0,12},{1,13},{2,14},{3,15},{4,0},{5,1},{6,2},{7,3},{8,4},{9,5},{1... | collective-permute-start | bytes 1277960 | tf_op jit(solution)/shard_map/ppermute | solution.py:29
  99.6 8.9 %collective-permute-start.27 = (bf16[128,1024]{1,0:T(8,128)(2,1)S(1)}, bf16[128,1024]{1,0:T(8,128)(2,1)S(1)}, u32[]{:S(2)}, u32[]{:S(2)}) collective-permute-start(bf16[128,1024]{1,0:T(8,128)(2,1)S(1)} %collective-permute-done.20.refs_3_), channel_id=1, source_target_pairs={{0,64},{1,65},{2,66},{3,67},{4,68},{5,69},{6,70},{7,71},{8,72},{9,... | collective-permute-start | bytes 786440 | tf_op jit(solution)/shard_map/ppermute | solution.py:29
  100.4 8.2 %collective-permute-start.28 = (bf16[128,1024]{1,0:T(8,128)(2,1)S(1)}, bf16[128,1024]{1,0:T(8,128)(2,1)S(1)}, u32[]{:S(2)}, u32[]{:S(2)}) collective-permute-start(bf16[128,1024]{1,0:T(8,128)(2,1)S(1)} %collective-permute-done.19.refs_8_), channel_id=1, source_target_pairs={{0,192},{1,193},{2,194},{3,195},{4,196},{5,197},{6,198},{7,199},{8... | collective-permute-start | bytes 786440 | tf_op jit(solution)/shard_map/ppermute | solution.py:29
  109.9 6.8 %collective-permute-start.31 = (f32[104,1664]{1,0:T(8,128)S(1)}, f32[104,1664]{1,0:T(8,128)S(1)}, u32[]{:S(2)}, u32[]{:S(2)}) collective-permute-start(f32[104,1664]{1,0:T(8,128)S(1)} %get-tuple-element.69), channel_id=1, source_target_pairs={{0,1},{1,0},{2,3},{3,2},{4,5},{5,4},{6,7},{7,6},{8,9},{9,8},{10,11... | collective-permute-start | bytes 2076680 | tf_op jit(solution)/shard_map/ppermute | solution.py:29

commit v4 on v3

--- a/solution.py
+++ b/solution.py
@@ -276,10 +276,13 @@
         (hidden, other_zh), (second, next_zl), (second, up_x), (second, down_x),
         (normed_1, up_y), (normed_1, down_y), slow=1,
     )
-    x_below_3, x_above_3, x_below_2, x_above_2, n_far, n_far_1 = step(
-        (fourth, up_x), (fourth, down_x), (third, up_x), (third, down_x),
-        (n_below, up_y), (n_above_1, down_y)
-    )
+    pair = jnp.concatenate([third, fourth], axis=0)
+    x_below, x_above, n_far, n_far_1, h_far = step(
+        (pair, up_x), (pair, down_x), (n_below, up_y), (n_above_1, down_y), (h_below, up_y)
+    )
+    tokens = normed.shape[0]
+    x_below_2, x_below_3 = x_below[:tokens], x_below[tokens:]
+    x_above_2, x_above_3 = x_above[:tokens], x_above[tokens:]
     own = rows_panel(
         [normed, n_below, n_above, n_far, normed_1, n_below_1, n_above_1, n_far_1]
     )
@@ -290,12 +293,14 @@
     early = [first, x_below_0, x_above_0, x_far_0, second, x_below_1, x_above_1, x_far_1]
     partial = in_product(own, other, early, (0, 1), scale)
     terms = down_terms(
-        [hidden, h_below, h_above, hidden_1, h_below_1, h_above_1], scale
-    )
-    h_far_1, h_far, x_far_2, x_far_3 = step(
-        (h_above_1, down_y), (h_below, up_y), (x_below_2, up_x), (x_above_3, down_x)
-    )
-    *held, partial = step.hold(h_far, h_far_1, partial)
+        [hidden, h_below, h_above, h_far, hidden_1, h_below_1, h_above_1], scale
+    )
+    half = tokens // 2
+    *far, x_far_2, x_far_3 = step(
+        (h_above_1[:half], down_y), (h_below_1[half:], up_y),
+        (x_below_2, up_x), (x_above_3, down_x)
+    )
+    *held, partial = step.hold(*far, partial)
     mine, theirs = down_terms(held, scale, terms)
     h_down = mine + send(theirs, other_core)
     late = [third, x_below_2, x_above_2, x_far_2, fourth, x_below_3, x_above_3, x_far_3]

time: 118 us -> 120 us (1.017)
  waiting for transfers between devices: 42.5 us -> 46.6 us
  starting transfers between devices: 60.3 us -> 57.7 us
    ppermute x32 -> x31, waiting for transfers between devices: 42.5 us -> 46.6 us  [send(): return lax.ppermute(value, ('tp', 'hb'), pairs)]
    ppermute x32 -> x31, starting transfers between devices: 60.3 us -> 57.7 us  [send(): return lax.ppermute(value, ('tp', 'hb'), pairs)]
  transfers between devices with their start and end apart: 32 -> 31, of which waited for: 12 -> 12; matrix products, arithmetic and copies ran while one was open for 0% -> 0% of each run, Pallas kernels for 9% -> 10%
where the time goes in v4:
time: 120 us
  starting transfers between devices  57.7 us (48%)
  waiting for transfers between devices  46.6 us (39%)
  Pallas kernels  12.7 us (11%)
    ppermute x31, starting transfers between devices, send(): return lax.ppermute(value, ('tp', 'hb'), pairs)  57.7 us
    ppermute x31, waiting for transfers between devices, send(): return lax.ppermute(value, ('tp', 'hb'), pairs)  46.6 us
    pallas_call x2, Pallas kernels, in_product(): pl.pallas_call(functools.partial(in_kernel, steps, scale), out_shape=jax....  7.67 us
    pallas_call x2, Pallas kernels, down_terms(): pl.pallas_call(functools.partial(down_kernel, len(blocks), scale), out_sh...  4.79 us
  transfers between devices with their start and end apart: 31, of which 12 were waited for; matrix products, arithmetic and copies ran while one was open for 0% of the time, Pallas kernels for 10%

profile of v4, /device:TPU:33, one launch (start us, length us, event | category | flops | bytes accessed | tf_op | source)
XLA Modules:
  0.0 119.8 jit_solution(12245237073350928442)
XLA Ops:
  0.6 0.0 copy-start
  0.6 1.4 %collective-permute-start.2 = (bf16[128,1664]{1,0:T(8,128)(2,1)}, bf16[128,1664]{1,0:T(8,128)(2,1)S(1)}, u32[]{:S(2)}, u32[]{:S(2)}) collective-permute-start(bf16[128,1664]{1,0:T(8,128)(2,1)} %refs_0_.3), channel_id=1, source_target_pairs={{0,4},{1,5},{2,6},{3,7},{4,8},{5,9},{6,10},{7,11},{8,12},{9,13},{1... | collective-permute-start | bytes 1277960 | tf_op jit(solution)/shard_map/ppermute | solution.py:29
  2.0 1.5 %collective-permute-start.3 = (bf16[128,1664]{1,0:T(8,128)(2,1)}, bf16[128,1664]{1,0:T(8,128)(2,1)S(1)}, u32[]{:S(2)}, u32[]{:S(2)}) collective-permute-start(bf16[128,1664]{1,0:T(8,128)(2,1)} %refs_0_.3), channel_id=1, source_target_pairs={{0,12},{1,13},{2,14},{3,15},{4,0},{5,1},{6,2},{7,3},{8,4},{9,5},{1... | collective-permute-start | bytes 1277960 | tf_op jit(solution)/shard_map/ppermute | solution.py:29
  3.5 6.0 %collective-permute-start.1 = (bf16[128,1024]{1,0:T(8,128)(2,1)}, bf16[128,1024]{1,0:T(8,128)(2,1)S(1)}, u32[]{:S(2)}, u32[]{:S(2)}) collective-permute-start(bf16[128,1024]{1,0:T(8,128)(2,1)} %refs_0_.2), channel_id=1, source_target_pairs={{0,2},{1,3},{2,0},{3,1},{4,6},{5,7},{6,4},{7,5},{8,10},{9,11},{10,... | collective-permute-start | bytes 786440 | tf_op jit(solution)/shard_map/ppermute | solution.py:29
  9.6 2.6 %collective-permute-start = (bf16[128,1024]{1,0:T(8,128)(2,1)}, bf16[128,1024]{1,0:T(8,128)(2,1)S(1)}, u32[]{:S(2)}, u32[]{:S(2)}) collective-permute-start(bf16[128,1024]{1,0:T(8,128)(2,1)} %refs_0_.2), channel_id=1, source_target_pairs={{0,0},{1,16},{2,48},{3,32},{4,64},{5,80},{6,112},{7,96},{8,128},{9... | collective-permute-start | bytes 786440 | tf_op jit(solution)/shard_map/ppermute | solution.py:29
  12.2 7.3 %collective-permute-done.1.refs_4_ = bf16[128,1024]{1,0:T(8,128)(2,1)S(1)} collective-permute-done((bf16[128,1024]{1,0:T(8,128)(2,1)}, bf16[128,1024]{1,0:T(8,128)(2,1)S(1)}, u32[]{:S(2)}, u32[]{:S(2)}) %collective-permute-start.1) | collective-permute-done | bytes 262176 | tf_op jit(solution)/shard_map/ppermute | solution.py:29
  19.5 2.9 %collective-permute-done.refs_2_ = bf16[128,1024]{1,0:T(8,128)(2,1)S(1)} collective-permute-done((bf16[128,1024]{1,0:T(8,128)(2,1)}, bf16[128,1024]{1,0:T(8,128)(2,1)S(1)}, u32[]{:S(2)}, u32[]{:S(2)}) %collective-permute-start) | collective-permute-done | bytes 262176 | tf_op jit(solution)/shard_map/ppermute | solution.py:29
  22.4 0.0 collective-permute-done.2.refs_1_
  22.4 1.7 %collective-permute-start.4 = (bf16[128,1024]{1,0:T(8,128)(2,1)}, bf16[128,1024]{1,0:T(8,128)(2,1)S(1)}, u32[]{:S(2)}, u32[]{:S(2)}) collective-permute-start(bf16[128,1024]{1,0:T(8,128)(2,1)} %refs_0_.2), channel_id=1, source_target_pairs={{0,4},{1,5},{2,6},{3,7},{4,8},{5,9},{6,10},{7,11},{8,12},{9,13},{1... | collective-permute-start | bytes 786440 | tf_op jit(solution)/shard_map/ppermute | solution.py:29
  24.1 3.1 %collective-permute-start.7 = (bf16[128,1024]{1,0:T(8,128)(2,1)S(1)}, bf16[128,1024]{1,0:T(8,128)(2,1)S(1)}, u32[]{:S(2)}, u32[]{:S(2)}) collective-permute-start(bf16[128,1024]{1,0:T(8,128)(2,1)S(1)} %collective-permute-done.refs_2_), channel_id=1, source_target_pairs={{0,32},{1,33},{2,34},{3,35},{4,36},{5,37},{6,38},{7,39},{8,40},{9,... | collective-permute-start | bytes 786440 | tf_op jit(solution)/shard_map/ppermute | solution.py:29
  27.3 1.6 %collective-permute-start.8 = (bf16[128,1024]{1,0:T(8,128)(2,1)S(1)}, bf16[128,1024]{1,0:T(8,128)(2,1)S(1)}, u32[]{:S(2)}, u32[]{:S(2)}) collective-permute-start(bf16[128,1024]{1,0:T(8,128)(2,1)S(1)} %collective-permute-done.refs_2_), channel_id=1, source_target_pairs={{0,64},{1,65},{2,66},{3,67},{4,68},{5,69},{6,70},{7,71},{8,72},{9,... | collective-permute-start | bytes 786440 | tf_op jit(solution)/shard_map/ppermute | solution.py:29
  28.9 2.6 %collective-permute-start.5 = (bf16[128,1024]{1,0:T(8,128)(2,1)}, bf16[128,1024]{1,0:T(8,128)(2,1)S(1)}, u32[]{:S(2)}, u32[]{:S(2)}) collective-permute-start(bf16[128,1024]{1,0:T(8,128)(2,1)} %refs_0_.2), channel_id=1, source_target_pairs={{0,12},{1,13},{2,14},{3,15},{4,0},{5,1},{6,2},{7,3},{8,4},{9,5},{1... | collective-permute-start | bytes 786440 | tf_op jit(solution)/shard_map/ppermute | solution.py:29
  31.4 4.0 %collective-permute-start.6 = (bf16[128,1024]{1,0:T(8,128)(2,1)S(1)}, bf16[128,1024]{1,0:T(8,128)(2,1)S(1)}, u32[]{:S(2)}, u32[]{:S(2)}) collective-permute-start(bf16[128,1024]{1,0:T(8,128)(2,1)S(1)} %collective-permute-done.refs_2_), channel_id=1, source_target_pairs={{0,16},{1,17},{2,18},{3,19},{4,20},{5,21},{6,22},{7,23},{8,24},{9,... | collective-permute-start | bytes 786440 | tf_op jit(solution)/shard_map/ppermute | solution.py:29
  35.5 1.5 %collective-permute-start.9 = (bf16[128,1024]{1,0:T(8,128)(2,1)S(1)}, bf16[128,1024]{1,0:T(8,128)(2,1)S(1)}, u32[]{:S(2)}, u32[]{:S(2)}) collective-permute-start(bf16[128,1024]{1,0:T(8,128)(2,1)S(1)} %collective-permute-done.refs_2_), channel_id=1, source_target_pairs={{0,192},{1,193},{2,194},{3,195},{4,196},{5,197},{6,198},{7,199},{8... | collective-permute-start | bytes 786440 | tf_op jit(solution)/shard_map/ppermute | solution.py:29
  37.0 1.3 %collective-permute-done.8.refs_3_ = bf16[128,1024]{1,0:T(8,128)(2,1)S(1)} collective-permute-done((bf16[128,1024]{1,0:T(8,128)(2,1)S(1)}, bf16[128,1024]{1,0:T(8,128)(2,1)S(1)}, u32[]{:S(2)}, u32[]{:S(2)}) %collective-permute-start.8) | collective-permute-done | bytes 262176 | tf_op jit(solution)/shard_map/ppermute | solution.py:29
  38.3 5.9 %collective-permute-done.6.refs_6_ = bf16[128,1024]{1,0:T(8,128)(2,1)S(1)} collective-permute-done((bf16[128,1024]{1,0:T(8,128)(2,1)S(1)}, bf16[128,1024]{1,0:T(8,128)(2,1)S(1)}, u32[]{:S(2)}, u32[]{:S(2)}) %collective-permute-start.6) | collective-permute-done | bytes 262176 | tf_op jit(solution)/shard_map/ppermute | solution.py:29
  44.2 3.1 %collective-permute-start.10 = (bf16[128,1024]{1,0:T(8,128)(2,1)S(1)}, bf16[128,1024]{1,0:T(8,128)(2,1)S(1)}, u32[]{:S(2)}, u32[]{:S(2)}) collective-permute-start(bf16[128,1024]{1,0:T(8,128)(2,1)S(1)} %collective-permute-done.6.refs_6_), channel_id=1, source_target_pairs={{0,16},{1,17},{2,18},{3,19},{4,20},{5,21},{6,22},{7,23},{8,24},{9,... | collective-permute-start | bytes 786440 | tf_op jit(solution)/shard_map/ppermute | solution.py:29
  47.3 2.6 %collective-permute-start.13 = (bf16[128,1024]{1,0:T(8,128)(2,1)S(1)}, bf16[128,1024]{1,0:T(8,128)(2,1)S(1)}, u32[]{:S(2)}, u32[]{:S(2)}) collective-permute-start(bf16[128,1024]{1,0:T(8,128)(2,1)S(1)} %collective-permute-done.6.refs_6_), channel_id=1, source_target_pairs={{0,192},{1,193},{2,194},{3,195},{4,196},{5,197},{6,198},{7,199},{8... | collective-permute-start | bytes 786440 | tf_op jit(solution)/shard_map/ppermute | solution.py:29
  49.9 0.1 collective-permute-start.11
  50.0 1.3 %collective-permute-start.14 = (bf16[128,1024]{1,0:T(8,128)(2,1)S(1)}, bf16[128,1024]{1,0:T(8,128)(2,1)S(1)}, u32[]{:S(2)}, u32[]{:S(2)}) collective-permute-start(bf16[128,1024]{1,0:T(8,128)(2,1)S(1)} %collective-permute-done.1.refs_4_), channel_id=1, source_target_pairs={{0,4},{1,5},{2,6},{3,7},{4,8},{5,9},{6,10},{7,11},{8,12},{9,13},{1... | collective-permute-start | bytes 786440 | tf_op jit(solution)/shard_map/ppermute | solution.py:29
  51.4 0.1 collective-permute-done.10.refs_2_
  51.5 1.7 %collective-permute-done.13.refs_8_ = bf16[128,1024]{1,0:T(8,128)(2,1)S(1)} collective-permute-done((bf16[128,1024]{1,0:T(8,128)(2,1)S(1)}, bf16[128,1024]{1,0:T(8,128)(2,1)S(1)}, u32[]{:S(2)}, u32[]{:S(2)}) %collective-permute-start.13) | collective-permute-done | bytes 262176 | tf_op jit(solution)/shard_map/ppermute | solution.py:29
  53.2 2.2 %collective-permute-done.11.refs_6_ = bf16[128,1024]{1,0:T(8,128)(2,1)S(1)} collective-permute-done((bf16[128,1024]{1,0:T(8,128)(2,1)S(1)}, bf16[128,1024]{1,0:T(8,128)(2,1)S(1)}, u32[]{:S(2)}, u32[]{:S(2)}) %collective-permute-start.11) | collective-permute-done | bytes 262176 | tf_op jit(solution)/shard_map/ppermute | solution.py:29
  55.4 1.0 collective-permute-done.12.refs_7_
  56.5 1.3 %collective-permute-start.15 = (bf16[128,1024]{1,0:T(8,128)(2,1)S(1)}, bf16[128,1024]{1,0:T(8,128)(2,1)S(1)}, u32[]{:S(2)}, u32[]{:S(2)}) collective-permute-start(bf16[128,1024]{1,0:T(8,128)(2,1)S(1)} %collective-permute-done.4.refs_1_), channel_id=1, source_target_pairs={{0,4},{1,5},{2,6},{3,7},{4,8},{5,9},{6,10},{7,11},{8,12},{9,13},{1... | collective-permute-start | bytes 786440 | tf_op jit(solution)/shard_map/ppermute | solution.py:29
  57.8 2.7 %collective-permute-start.19 = (bf16[256,1024]{1,0:T(8,128)(2,1)S(1)}, bf16[256,1024]{1,0:T(8,128)(2,1)S(1)}, u32[]{:S(2)}, u32[]{:S(2)}) collective-permute-start(bf16[256,1024]{1,0:T(8,128)(2,1)S(1)} %pad_maximum_fusion), channel_id=1, source_target_pairs={{0,192},{1,193},{2,194},{3,195},{4,196},{5,197},{6,198},{7,199},{8... | collective-permute-start | bytes 1572872 | tf_op jit(solution)/shard_map/ppermute | solution.py:29
  60.5 5.1 %collective-permute-start.17 = (bf16[128,1664]{1,0:T(8,128)(2,1)}, bf16[128,1664]{1,0:T(8,128)(2,1)S(1)}, u32[]{:S(2)}, u32[]{:S(2)}) collective-permute-start(bf16[128,1664]{1,0:T(8,128)(2,1)} %refs_0_.3), channel_id=1, source_target_pairs={{0,2},{1,3},{2,0},{3,1},{4,6},{5,7},{6,4},{7,5},{8,10},{9,11},{10,... | collective-permute-start | bytes 1277960 | tf_op jit(solution)/shard_map/ppermute | solution.py:29
  65.6 0.0 collective-permute-start.20
  65.6 2.7 %collective-permute-start.16 = (bf16[128,1024]{1,0:T(8,128)(2,1)S(1)}, bf16[128,1024]{1,0:T(8,128)(2,1)S(1)}, u32[]{:S(2)}, u32[]{:S(2)}) collective-permute-start(bf16[128,1024]{1,0:T(8,128)(2,1)S(1)} %collective-permute-done.11.refs_6_), channel_id=1, source_target_pairs={{0,12},{1,13},{2,14},{3,15},{4,0},{5,1},{6,2},{7,3},{8,4},{9,5},{1... | collective-permute-start | bytes 786440 | tf_op jit(solution)/shard_map/ppermute | solution.py:29
  68.3 3.8 %collective-permute-done.16.refs_7_ = bf16[128,1024]{1,0:T(8,128)(2,1)S(1)} collective-permute-done((bf16[128,1024]{1,0:T(8,128)(2,1)S(1)}, bf16[128,1024]{1,0:T(8,128)(2,1)S(1)}, u32[]{:S(2)}, u32[]{:S(2)}) %collective-permute-start.16) | collective-permute-done | bytes 262176 | tf_op jit(solution)/shard_map/ppermute | solution.py:29
  72.0 0.9 copy-done.1
  73.0 0.2 shard_map.41.refs_0_
  73.2 10.8 %collective-permute-done.17.refs_4_ = bf16[128,1664]{1,0:T(8,128)(2,1)S(1)} collective-permute-done((bf16[128,1664]{1,0:T(8,128)(2,1)}, bf16[128,1664]{1,0:T(8,128)(2,1)S(1)}, u32[]{:S(2)}, u32[]{:S(2)}) %collective-permute-start.17) | collective-permute-done | bytes 426016 | tf_op jit(solution)/shard_map/ppermute | solution.py:29
  84.1 1.7 %collective-permute-start.21 = (bf16[8,128,1024]{2,1,0:T(8,128)(2,1)S(1)}, bf16[8,128,1024]{2,1,0:T(8,128)(2,1)S(1)}, u32[]{:S(2)}, u32[]{:S(2)}) collective-permute-start(bf16[8,128,1024]{2,1,0:T(8,128)(2,1)S(1)} %shard_map.41.refs_0_), channel_id=1, source_target_pairs={{0,1},{1,0},{2,3},{3,2},{4,5},{5,4},{6,7},{7,6},{8,9},{9,8},{10,11... | collective-permute-start | bytes 6291464 | tf_op jit(solution)/shard_map/ppermute | solution.py:29
  85.8 1.6 %collective-permute-start.22 = (bf16[128,1664]{1,0:T(8,128)(2,1)S(1)}, bf16[128,1664]{1,0:T(8,128)(2,1)S(1)}, u32[]{:S(2)}, u32[]{:S(2)}) collective-permute-start(bf16[128,1664]{1,0:T(8,128)(2,1)S(1)} %collective-permute-done.17.refs_4_), channel_id=1, source_target_pairs={{0,12},{1,13},{2,14},{3,15},{4,0},{5,1},{6,2},{7,3},{8,4},{9,5},{1... | collective-permute-start | bytes 1277960 | tf_op jit(solution)/shard_map/ppermute | solution.py:29
  87.4 2.7 %collective-permute-start.25 = (bf16[128,1024]{1,0:T(8,128)(2,1)S(1)}, bf16[128,1024]{1,0:T(8,128)(2,1)S(1)}, u32[]{:S(2)}, u32[]{:S(2)}) collective-permute-start(bf16[128,1024]{1,0:T(8,128)(2,1)S(1)} %collective-permute-done.13.refs_8_), channel_id=1, source_target_pairs={{0,192},{1,193},{2,194},{3,195},{4,196},{5,197},{6,198},{7,199},{8... | collective-permute-start | bytes 786440 | tf_op jit(solution)/shard_map/ppermute | solution.py:29
  90.2 7.0 %collective-permute-done.22.refs_6_ = bf16[128,1664]{1,0:T(8,128)(2,1)S(1)} collective-permute-done((bf16[128,1664]{1,0:T(8,128)(2,1)S(1)}, bf16[128,1664]{1,0:T(8,128)(2,1)S(1)}, u32[]{:S(2)}, u32[]{:S(2)}) %collective-permute-start.22) | collective-permute-done | bytes 426016 | tf_op jit(solution)/shard_map/ppermute | solution.py:29
  97.2 2.5 %collective-permute-done.23.refs_5_ = bf16[128,1664]{1,0:T(8,128)(2,1)S(1)} collective-permute-done((bf16[128,1664]{1,0:T(8,128)(2,1)S(1)}, bf16[128,1664]{1,0:T(8,128)(2,1)S(1)}, u32[]{:S(2)}, u32[]{:S(2)}) %collective-permute-start.23) | collective-permute-done | bytes 426016 | tf_op jit(solution)/shard_map/ppermute | solution.py:29
  99.7 0.1 collective-permute-start.26
  99.8 2.7 %collective-permute-start.27 = (bf16[128,1024]{1,0:T(8,128)(2,1)S(1)}, bf16[128,1024]{1,0:T(8,128)(2,1)S(1)}, u32[]{:S(2)}, u32[]{:S(2)}) collective-permute-start(bf16[128,1024]{1,0:T(8,128)(2,1)S(1)} %get-tuple-element.58.refs_8_), channel_id=1, source_target_pairs={{0,192},{1,193},{2,194},{3,195},{4,196},{5,197},{6,198},{7,199},{8... | collective-permute-start | bytes 786440 | tf_op jit(solution)/shard_map/ppermute | solution.py:29
  102.5 0.4 collective-permute-start.28
  102.8 1.1 collective-permute-start.29
  104.0 3.5 %shard_map.44 = (f32[104,1664]{1,0:T(8,128)S(1)}, f32[104,1664]{1,0:T(8,128)S(1)}) custom-call(bf16[128,1664]{1,0:T(8,128)(2,1)S(1)} %copy-done, bf16[128,1664]{1,0:T(8,128)(2,1)S(1)} %collective-permute-done.2.refs_1_, bf16[128,1664]{1,0:T(8,128)(2,1)S(1)} %collective-permute-done.3.refs_2_, bf16[128,1664]{1,0:T(8,128)(2,1)S(1)} %collective-permute-done.20.refs_3_, ...), custom_call_target="tpu_custom_call" | custom-call | flops 763363328 | bytes 6291456 | tf_op jit(solution)/shard_map/pallas_call | solution.py:247
  107.5 3.2 %shard_map.42.refs_10_ = f32[1024,1024]{1,0:T(8,128)S(1)} custom-call(bf16[8,128,1024]{2,1,0:T(8,128)(2,1)S(1)} %shard_map.41.refs_0_, bf16[8,128,1024]{2,1,0:T(8,128)(2,1)S(1)} %collective-permute-done.21.refs_1_, bf16[128,1024]{1,0:T(8,128)(2,1)S(1)} %collective-permute-done.refs_2_, bf16[128,1024]{1,0:T(8,128)(2,1)S(1)} %collective-permute-done.8.refs_3_, ...), custom_call_target="tpu_custom_call" | custom-call | flops 2147483648 | bytes 8388608 | tf_op jit(solution)/shard_map/pallas_call | solution.py:187
  110.7 1.3 %shard_map.45 = (f32[104,1664]{1,0:T(8,128)S(1)}, f32[104,1664]{1,0:T(8,128)S(1)}) custom-call(bf16[64,1664]{1,0:T(8,128)(2,1)S(1)} %collective-permute-done.28.refs_0_, bf16[64,1664]{1,0:T(8,128)(2,1)S(1)} %collective-permute-done.29.refs_1_, f32[104,1664]{1,0:T(8,128)S(1)} %get-tuple-element.64.refs_2_, f32[104,1664]{1,0:T(8,128)S(1)} %get-tuple-element.65.refs_3_), custom_call_target="tpu_custom_call" | custom-call | flops 109051904 | bytes 6291456 | tf_op jit(solution)/shard_map/pallas_call | solution.py:247
  112.0 2.4 %collective-permute-start.30 = (f32[104,1664]{1,0:T(8,128)S(1)}, f32[104,1664]{1,0:T(8,128)S(1)}, u32[]{:S(2)}, u32[]{:S(2)}) collective-permute-start(f32[104,1664]{1,0:T(8,128)S(1)} %get-tuple-element.67), channel_id=1, source_target_pairs={{0,1},{1,0},{2,3},{3,2},{4,5},{5,4},{6,7},{7,6},{8,9},{9,8},{10,11... | collective-permute-start | bytes 2076680 | tf_op jit(solution)/shard_map/ppermute | solution.py:29
  114.4 4.5 %shard_map.43 = f32[1024,1024]{1,0:T(8,128)} custom-call(bf16[8,128,1024]{2,1,0:T(8,128)(2,1)S(1)} %shard_map.41.refs_0_, bf16[8,128,1024]{2,1,0:T(8,128)(2,1)S(1)} %collective-permute-done.21.refs_1_, bf16[128,1024]{1,0:T(8,128)(2,1)S(1)} %collective-permute-done.10.refs_2_, bf16[128,1024]{1,0:T(8,128)(2,1)S(1)} %get-tuple-element.57.refs_3_, ...), custom_call_target="tpu_custom_call" | custom-call | flops 2147483648 | bytes 8388608 | tf_op jit(solution)/shard_map/pallas_call | solution.py:187
  118.9 0.9 add.3
  (29 shorter events, 0.2 us)
Async XLA Ops:
  0.6 103.3 %copy-start = (bf16[128,1664]{1,0:T(8,128)(2,1)S(1)}, bf16[128,1664]{1,0:T(8,128)(2,1)}, u32[]{:S(2)}) copy-start(bf16[128,1664]{1,0:T(8,128)(2,1)} %refs_0_.3) | copy-start | bytes 1277956
  0.6 21.8 %collective-permute-start.2 = (bf16[128,1664]{1,0:T(8,128)(2,1)}, bf16[128,1664]{1,0:T(8,128)(2,1)S(1)}, u32[]{:S(2)}, u32[]{:S(2)}) collective-permute-start(bf16[128,1664]{1,0:T(8,128)(2,1)} %refs_0_.3), channel_id=1, source_target_pairs={{0,4},{1,5},{2,6},{3,7},{4,8},{5,9},{6,10},{7,11},{8,12},{9,13},{1... | collective-permute-start | bytes 1277960 | tf_op jit(solution)/shard_map/ppermute | solution.py:29
  2.0 20.4 %collective-permute-start.3 = (bf16[128,1664]{1,0:T(8,128)(2,1)}, bf16[128,1664]{1,0:T(8,128)(2,1)S(1)}, u32[]{:S(2)}, u32[]{:S(2)}) collective-permute-start(bf16[128,1664]{1,0:T(8,128)(2,1)} %refs_0_.3), channel_id=1, source_target_pairs={{0,12},{1,13},{2,14},{3,15},{4,0},{5,1},{6,2},{7,3},{8,4},{9,5},{1... | collective-permute-start | bytes 1277960 | tf_op jit(solution)/shard_map/ppermute | solution.py:29
  3.5 16.0 %collective-permute-start.1 = (bf16[128,1024]{1,0:T(8,128)(2,1)}, bf16[128,1024]{1,0:T(8,128)(2,1)S(1)}, u32[]{:S(2)}, u32[]{:S(2)}) collective-permute-start(bf16[128,1024]{1,0:T(8,128)(2,1)} %refs_0_.2), channel_id=1, source_target_pairs={{0,2},{1,3},{2,0},{3,1},{4,6},{5,7},{6,4},{7,5},{8,10},{9,11},{10,... | collective-permute-start | bytes 786440 | tf_op jit(solution)/shard_map/ppermute | solution.py:29
  9.6 12.9 %collective-permute-start = (bf16[128,1024]{1,0:T(8,128)(2,1)}, bf16[128,1024]{1,0:T(8,128)(2,1)S(1)}, u32[]{:S(2)}, u32[]{:S(2)}) collective-permute-start(bf16[128,1024]{1,0:T(8,128)(2,1)} %refs_0_.2), channel_id=1, source_target_pairs={{0,0},{1,16},{2,48},{3,32},{4,64},{5,80},{6,112},{7,96},{8,128},{9... | collective-permute-start | bytes 786440 | tf_op jit(solution)/shard_map/ppermute | solution.py:29
  22.4 13.1 %collective-permute-start.4 = (bf16[128,1024]{1,0:T(8,128)(2,1)}, bf16[128,1024]{1,0:T(8,128)(2,1)S(1)}, u32[]{:S(2)}, u32[]{:S(2)}) collective-permute-start(bf16[128,1024]{1,0:T(8,128)(2,1)} %refs_0_.2), channel_id=1, source_target_pairs={{0,4},{1,5},{2,6},{3,7},{4,8},{5,9},{6,10},{7,11},{8,12},{9,13},{1... | collective-permute-start | bytes 786440 | tf_op jit(solution)/shard_map/ppermute | solution.py:29
  24.1 12.8 %collective-permute-start.7 = (bf16[128,1024]{1,0:T(8,128)(2,1)S(1)}, bf16[128,1024]{1,0:T(8,128)(2,1)S(1)}, u32[]{:S(2)}, u32[]{:S(2)}) collective-permute-start(bf16[128,1024]{1,0:T(8,128)(2,1)S(1)} %collective-permute-done.refs_2_), channel_id=1, source_target_pairs={{0,32},{1,33},{2,34},{3,35},{4,36},{5,37},{6,38},{7,39},{8,40},{9,... | collective-permute-start | bytes 786440 | tf_op jit(solution)/shard_map/ppermute | solution.py:29
  27.3 11.0 %collective-permute-start.8 = (bf16[128,1024]{1,0:T(8,128)(2,1)S(1)}, bf16[128,1024]{1,0:T(8,128)(2,1)S(1)}, u32[]{:S(2)}, u32[]{:S(2)}) collective-permute-start(bf16[128,1024]{1,0:T(8,128)(2,1)S(1)} %collective-permute-done.refs_2_), channel_id=1, source_target_pairs={{0,64},{1,65},{2,66},{3,67},{4,68},{5,69},{6,70},{7,71},{8,72},{9,... | collective-permute-start | bytes 786440 | tf_op jit(solution)/shard_map/ppermute | solution.py:29
  28.9 9.4 %collective-permute-start.5 = (bf16[128,1024]{1,0:T(8,128)(2,1)}, bf16[128,1024]{1,0:T(8,128)(2,1)S(1)}, u32[]{:S(2)}, u32[]{:S(2)}) collective-permute-start(bf16[128,1024]{1,0:T(8,128)(2,1)} %refs_0_.2), channel_id=1, source_target_pairs={{0,12},{1,13},{2,14},{3,15},{4,0},{5,1},{6,2},{7,3},{8,4},{9,5},{1... | collective-permute-start | bytes 786440 | tf_op jit(solution)/shard_map/ppermute | solution.py:29
  31.4 12.8 %collective-permute-start.6 = (bf16[128,1024]{1,0:T(8,128)(2,1)S(1)}, bf16[128,1024]{1,0:T(8,128)(2,1)S(1)}, u32[]{:S(2)}, u32[]{:S(2)}) collective-permute-start(bf16[128,1024]{1,0:T(8,128)(2,1)S(1)} %collective-permute-done.refs_2_), channel_id=1, source_target_pairs={{0,16},{1,17},{2,18},{3,19},{4,20},{5,21},{6,22},{7,23},{8,24},{9,... | collective-permute-start | bytes 786440 | tf_op jit(solution)/shard_map/ppermute | solution.py:29
  35.5 8.7 %collective-permute-start.9 = (bf16[128,1024]{1,0:T(8,128)(2,1)S(1)}, bf16[128,1024]{1,0:T(8,128)(2,1)S(1)}, u32[]{:S(2)}, u32[]{:S(2)}) collective-permute-start(bf16[128,1024]{1,0:T(8,128)(2,1)S(1)} %collective-permute-done.refs_2_), channel_id=1, source_target_pairs={{0,192},{1,193},{2,194},{3,195},{4,196},{5,197},{6,198},{7,199},{8... | collective-permute-start | bytes 786440 | tf_op jit(solution)/shard_map/ppermute | solution.py:29
  44.2 7.3 %collective-permute-start.10 = (bf16[128,1024]{1,0:T(8,128)(2,1)S(1)}, bf16[128,1024]{1,0:T(8,128)(2,1)S(1)}, u32[]{:S(2)}, u32[]{:S(2)}) collective-permute-start(bf16[128,1024]{1,0:T(8,128)(2,1)S(1)} %collective-permute-done.6.refs_6_), channel_id=1, source_target_pairs={{0,16},{1,17},{2,18},{3,19},{4,20},{5,21},{6,22},{7,23},{8,24},{9,... | collective-permute-start | bytes 786440 | tf_op jit(solution)/shard_map/ppermute | solution.py:29
  47.3 5.9 %collective-permute-start.13 = (bf16[128,1024]{1,0:T(8,128)(2,1)S(1)}, bf16[128,1024]{1,0:T(8,128)(2,1)S(1)}, u32[]{:S(2)}, u32[]{:S(2)}) collective-permute-start(bf16[128,1024]{1,0:T(8,128)(2,1)S(1)} %collective-permute-done.6.refs_6_), channel_id=1, source_target_pairs={{0,192},{1,193},{2,194},{3,195},{4,196},{5,197},{6,198},{7,199},{8... | collective-permute-start | bytes 786440 | tf_op jit(solution)/shard_map/ppermute | solution.py:29
  49.9 5.5 %collective-permute-start.11 = (bf16[128,1024]{1,0:T(8,128)(2,1)S(1)}, bf16[128,1024]{1,0:T(8,128)(2,1)S(1)}, u32[]{:S(2)}, u32[]{:S(2)}) collective-permute-start(bf16[128,1024]{1,0:T(8,128)(2,1)S(1)} %collective-permute-done.1.refs_4_), channel_id=1, source_target_pairs={{0,12},{1,13},{2,14},{3,15},{4,0},{5,1},{6,2},{7,3},{8,4},{9,5},{1... | collective-permute-start | bytes 786440 | tf_op jit(solution)/shard_map/ppermute | solution.py:29
  50.0 6.4 %collective-permute-start.12 = (bf16[128,1024]{1,0:T(8,128)(2,1)S(1)}, bf16[128,1024]{1,0:T(8,128)(2,1)S(1)}, u32[]{:S(2)}, u32[]{:S(2)}) collective-permute-start(bf16[128,1024]{1,0:T(8,128)(2,1)S(1)} %collective-permute-done.6.refs_6_), channel_id=1, source_target_pairs={{0,64},{1,65},{2,66},{3,67},{4,68},{5,69},{6,70},{7,71},{8,72},{9,... | collective-permute-start | bytes 786440 | tf_op jit(solution)/shard_map/ppermute | solution.py:29
  50.0 6.4 %collective-permute-start.14 = (bf16[128,1024]{1,0:T(8,128)(2,1)S(1)}, bf16[128,1024]{1,0:T(8,128)(2,1)S(1)}, u32[]{:S(2)}, u32[]{:S(2)}) collective-permute-start(bf16[128,1024]{1,0:T(8,128)(2,1)S(1)} %collective-permute-done.1.refs_4_), channel_id=1, source_target_pairs={{0,4},{1,5},{2,6},{3,7},{4,8},{5,9},{6,10},{7,11},{8,12},{9,13},{1... | collective-permute-start | bytes 786440 | tf_op jit(solution)/shard_map/ppermute | solution.py:29
  56.5 9.2 %collective-permute-start.15 = (bf16[128,1024]{1,0:T(8,128)(2,1)S(1)}, bf16[128,1024]{1,0:T(8,128)(2,1)S(1)}, u32[]{:S(2)}, u32[]{:S(2)}) collective-permute-start(bf16[128,1024]{1,0:T(8,128)(2,1)S(1)} %collective-permute-done.4.refs_1_), channel_id=1, source_target_pairs={{0,4},{1,5},{2,6},{3,7},{4,8},{5,9},{6,10},{7,11},{8,12},{9,13},{1... | collective-permute-start | bytes 786440 | tf_op jit(solution)/shard_map/ppermute | solution.py:29
  57.8 26.3 %collective-permute-start.18 = (bf16[256,1024]{1,0:T(8,128)(2,1)S(1)}, bf16[256,1024]{1,0:T(8,128)(2,1)S(1)}, u32[]{:S(2)}, u32[]{:S(2)}) collective-permute-start(bf16[256,1024]{1,0:T(8,128)(2,1)S(1)} %pad_maximum_fusion), channel_id=1, source_target_pairs={{0,64},{1,65},{2,66},{3,67},{4,68},{5,69},{6,70},{7,71},{8,72},{9,... | collective-permute-start | bytes 1572872 | tf_op jit(solution)/shard_map/ppermute | solution.py:29
  57.8 26.3 %collective-permute-start.19 = (bf16[256,1024]{1,0:T(8,128)(2,1)S(1)}, bf16[256,1024]{1,0:T(8,128)(2,1)S(1)}, u32[]{:S(2)}, u32[]{:S(2)}) collective-permute-start(bf16[256,1024]{1,0:T(8,128)(2,1)S(1)} %pad_maximum_fusion), channel_id=1, source_target_pairs={{0,192},{1,193},{2,194},{3,195},{4,196},{5,197},{6,198},{7,199},{8... | collective-permute-start | bytes 1572872 | tf_op jit(solution)/shard_map/ppermute | solution.py:29
  60.5 23.6 %collective-permute-start.17 = (bf16[128,1664]{1,0:T(8,128)(2,1)}, bf16[128,1664]{1,0:T(8,128)(2,1)S(1)}, u32[]{:S(2)}, u32[]{:S(2)}) collective-permute-start(bf16[128,1664]{1,0:T(8,128)(2,1)} %refs_0_.3), channel_id=1, source_target_pairs={{0,2},{1,3},{2,0},{3,1},{4,6},{5,7},{6,4},{7,5},{8,10},{9,11},{10,... | collective-permute-start | bytes 1277960 | tf_op jit(solution)/shard_map/ppermute | solution.py:29
  65.6 18.5 %collective-permute-start.20 = (bf16[128,1664]{1,0:T(8,128)(2,1)S(1)}, bf16[128,1664]{1,0:T(8,128)(2,1)S(1)}, u32[]{:S(2)}, u32[]{:S(2)}) collective-permute-start(bf16[128,1664]{1,0:T(8,128)(2,1)S(1)} %collective-permute-done.2.refs_1_), channel_id=1, source_target_pairs={{0,4},{1,5},{2,6},{3,7},{4,8},{5,9},{6,10},{7,11},{8,12},{9,13},{1... | collective-permute-start | bytes 1277960 | tf_op jit(solution)/shard_map/ppermute | solution.py:29
  65.6 6.4 %collective-permute-start.16 = (bf16[128,1024]{1,0:T(8,128)(2,1)S(1)}, bf16[128,1024]{1,0:T(8,128)(2,1)S(1)}, u32[]{:S(2)}, u32[]{:S(2)}) collective-permute-start(bf16[128,1024]{1,0:T(8,128)(2,1)S(1)} %collective-permute-done.11.refs_6_), channel_id=1, source_target_pairs={{0,12},{1,13},{2,14},{3,15},{4,0},{5,1},{6,2},{7,3},{8,4},{9,5},{1... | collective-permute-start | bytes 786440 | tf_op jit(solution)/shard_map/ppermute | solution.py:29
  72.0 0.9 copy-start.1
  84.1 15.6 %collective-permute-start.21 = (bf16[8,128,1024]{2,1,0:T(8,128)(2,1)S(1)}, bf16[8,128,1024]{2,1,0:T(8,128)(2,1)S(1)}, u32[]{:S(2)}, u32[]{:S(2)}) collective-permute-start(bf16[8,128,1024]{2,1,0:T(8,128)(2,1)S(1)} %shard_map.41.refs_0_), channel_id=1, source_target_pairs={{0,1},{1,0},{2,3},{3,2},{4,5},{5,4},{6,7},{7,6},{8,9},{9,8},{10,11... | collective-permute-start | bytes 6291464 | tf_op jit(solution)/shard_map/ppermute | solution.py:29
  85.8 11.4 %collective-permute-start.22 = (bf16[128,1664]{1,0:T(8,128)(2,1)S(1)}, bf16[128,1664]{1,0:T(8,128)(2,1)S(1)}, u32[]{:S(2)}, u32[]{:S(2)}) collective-permute-start(bf16[128,1664]{1,0:T(8,128)(2,1)S(1)} %collective-permute-done.17.refs_4_), channel_id=1, source_target_pairs={{0,12},{1,13},{2,14},{3,15},{4,0},{5,1},{6,2},{7,3},{8,4},{9,5},{1... | collective-permute-start | bytes 1277960 | tf_op jit(solution)/shard_map/ppermute | solution.py:29
  87.4 12.3 %collective-permute-start.23 = (bf16[128,1664]{1,0:T(8,128)(2,1)S(1)}, bf16[128,1664]{1,0:T(8,128)(2,1)S(1)}, u32[]{:S(2)}, u32[]{:S(2)}) collective-permute-start(bf16[128,1664]{1,0:T(8,128)(2,1)S(1)} %collective-permute-done.17.refs_4_), channel_id=1, source_target_pairs={{0,4},{1,5},{2,6},{3,7},{4,8},{5,9},{6,10},{7,11},{8,12},{9,13},{1... | collective-permute-start | bytes 1277960 | tf_op jit(solution)/shard_map/ppermute | solution.py:29
  87.4 12.3 %collective-permute-start.24 = (bf16[128,1024]{1,0:T(8,128)(2,1)S(1)}, bf16[128,1024]{1,0:T(8,128)(2,1)S(1)}, u32[]{:S(2)}, u32[]{:S(2)}) collective-permute-start(bf16[128,1024]{1,0:T(8,128)(2,1)S(1)} %collective-permute-done.8.refs_3_), channel_id=1, source_target_pairs={{0,64},{1,65},{2,66},{3,67},{4,68},{5,69},{6,70},{7,71},{8,72},{9,... | collective-permute-start | bytes 786440 | tf_op jit(solution)/shard_map/ppermute | solution.py:29
  87.4 12.3 %collective-permute-start.25 = (bf16[128,1024]{1,0:T(8,128)(2,1)S(1)}, bf16[128,1024]{1,0:T(8,128)(2,1)S(1)}, u32[]{:S(2)}, u32[]{:S(2)}) collective-permute-start(bf16[128,1024]{1,0:T(8,128)(2,1)S(1)} %collective-permute-done.13.refs_8_), channel_id=1, source_target_pairs={{0,192},{1,193},{2,194},{3,195},{4,196},{5,197},{6,198},{7,199},{8... | collective-permute-start | bytes 786440 | tf_op jit(solution)/shard_map/ppermute | solution.py:29
  99.7 11.0 %collective-permute-start.26 = (bf16[128,1024]{1,0:T(8,128)(2,1)S(1)}, bf16[128,1024]{1,0:T(8,128)(2,1)S(1)}, u32[]{:S(2)}, u32[]{:S(2)}) collective-permute-start(bf16[128,1024]{1,0:T(8,128)(2,1)S(1)} %get-tuple-element.57.refs_3_), channel_id=1, source_target_pairs={{0,64},{1,65},{2,66},{3,67},{4,68},{5,69},{6,70},{7,71},{8,72},{9,... | collective-permute-start | bytes 786440 | tf_op jit(solution)/shard_map/ppermute | solution.py:29
  99.8 10.9 %collective-permute-start.27 = (bf16[128,1024]{1,0:T(8,128)(2,1)S(1)}, bf16[128,1024]{1,0:T(8,128)(2,1)S(1)}, u32[]{:S(2)}, u32[]{:S(2)}) collective-permute-start(bf16[128,1024]{1,0:T(8,128)(2,1)S(1)} %get-tuple-element.58.refs_8_), channel_id=1, source_target_pairs={{0,192},{1,193},{2,194},{3,195},{4,196},{5,197},{6,198},{7,199},{8... | collective-permute-start | bytes 786440 | tf_op jit(solution)/shard_map/ppermute | solution.py:29
  102.5 8.2 %collective-permute-start.28 = (bf16[64,1664]{1,0:T(8,128)(2,1)S(1)}, bf16[64,1664]{1,0:T(8,128)(2,1)S(1)}, u32[]{:S(2)}, u32[]{:S(2)}) collective-permute-start(bf16[64,1664]{1,0:T(8,128)(2,1)S(1)} %slice.26), channel_id=1, source_target_pairs={{0,12},{1,13},{2,14},{3,15},{4,0},{5,1},{6,2},{7,3},{8,4},{9,5},{1... | collective-permute-start | bytes 638984 | tf_op jit(solution)/shard_map/ppermute | solution.py:29
  102.8 7.8 %collective-permute-start.29 = (bf16[64,1664]{1,0:T(8,128)(2,1)S(1)}, bf16[64,1664]{1,0:T(8,128)(2,1)S(1)}, u32[]{:S(2)}, u32[]{:S(2)}) collective-permute-start(bf16[64,1664]{1,0:T(8,128)(2,1)S(1)} %slice.27), channel_id=1, source_target_pairs={{0,4},{1,5},{2,6},{3,7},{4,8},{5,9},{6,10},{7,11},{8,12},{9,13},{1... | collective-permute-start | bytes 638984 | tf_op jit(solution)/shard_map/ppermute | solution.py:29
  112.0 6.9 %collective-permute-start.30 = (f32[104,1664]{1,0:T(8,128)S(1)}, f32[104,1664]{1,0:T(8,128)S(1)}, u32[]{:S(2)}, u32[]{:S(2)}) collective-permute-start(f32[104,1664]{1,0:T(8,128)S(1)} %get-tuple-element.67), channel_id=1, source_target_pairs={{0,1},{1,0},{2,3},{3,2},{4,5},{5,4},{6,7},{7,6},{8,9},{9,8},{10,11... | collective-permute-start | bytes 2076680 | tf_op jit(solution)/shard_map/ppermute | solution.py:29
